TPU v7x, 32 devices: a whole 2x2x4 slice. The times are simulated.
32 devices in a mesh: rows: 2 (over x), cols: 2 (over core), imgs: 8 (over z, y).
Axes of the slice: x: 2, y: 2, z: 4, core: 2. Of those that a mesh axis runs over, the one named last changes fastest.
Arguments:
- patches: bfloat16 [8, 30, 30, 768], P('imgs', 'rows', 'cols'), may hold values from -6 to 6
- patch_mask: int32 [8, 30, 30], P('imgs'), may hold values from 0 to 1, as said below
- norm1_gain: float32 [768], replicated, may hold values from 0.1 to 1.9
- norm1_shift: float32 [768], replicated, may hold values from -3 to 3
- qkv_weight: bfloat16 [768, 2304], replicated, may hold values from -0.21875 to 0.21875
- qv_bias: float32 [768, 2], replicated, may hold values from -3 to 3
- out_weight: bfloat16 [768, 768], replicated, may hold values from -1.25 to 1.25
- out_bias: float32 [768], replicated, may hold values from -3 to 3
- norm2_gain: float32 [768], replicated, may hold values from 0.1 to 1.9
- norm2_shift: float32 [768], replicated, may hold values from -3 to 3
- fc1_weight: bfloat16 [768, 3072], replicated, may hold values from -0.21875 to 0.21875
- fc1_bias: float32 [3072], replicated, may hold values from -3 to 3
- fc2_weight: bfloat16 [3072, 768], replicated, may hold values from -0.109375 to 0.109375
- fc2_bias: float32 [768], replicated, may hold values from -3 to 3
- cotangent: bfloat16 [8, 30, 30, 768], P('imgs', 'rows', 'cols'), may hold values from -6 to 6
Outputs:
- layer_out: bfloat16 [8, 30, 30, 768], P('imgs', 'rows', 'cols')
- patches_grad: bfloat16 [8, 30, 30, 768], P('imgs', 'rows', 'cols')
- norm1_gain_grad: float32 [768], P('imgs')
- norm1_shift_grad: float32 [768], P('imgs')
- qkv_weight_grad: float32 [768, 2304], P('imgs')
- qv_bias_grad: float32 [768, 2], P('imgs')
- out_weight_grad: float32 [768, 768], P('imgs')
- out_bias_grad: float32 [768], P('imgs')
- norm2_gain_grad: float32 [768], P('imgs')
- norm2_shift_grad: float32 [768], P('imgs')
- fc1_weight_grad: float32 [768, 3072], P('imgs')
- fc1_bias_grad: float32 [3072], P('imgs')
- fc2_weight_grad: float32 [3072, 768], P('imgs')
- fc2_bias_grad: float32 [768], P('imgs')
Inputs may be any that keep to these rules, and one draw needn't show every extreme that they name: For each image, patch_mask is 1 on a rectangle of h rows and w columns at the top left of the grid and 0 elsewhere, with 12 <= h, w <= 30; image 0 is whole and image 1 has h = w = 12.
All inputs are finite; a program needn't handle non-finite values.
Results may differ from a plain program's by a relative error of at most 0.012.
Values may be sent and summed in bfloat16 or wider, within the bound.
No kernel may reach another device: no remote copies, remote signals or barrier semaphores. Data moves between devices by JAX's collectives and lax.ppermute only.
A program may use at most 128 MiB of HBM per device.

v0:
```python
import functools

import jax
import jax.numpy as jnp
from jax import lax
from jax.experimental import pallas as pl
from jax.experimental.pallas import tpu as pltpu
from jax.sharding import PartitionSpec as P

HEADS = 12
NORM_EPS = 1e-06
MASKED_SCORE = -1e30
GROUP = ("rows", "cols")
BF = jnp.bfloat16
F32 = jnp.float32


def dot(left, right, dims):
    return lax.dot_general(left, right, (dims, ((), ())), preferred_element_type=F32)


def mm(left, right):
    return dot(left, right, ((1,), (0,)))


def mm_nt(left, right):
    return dot(left, right, ((1,), (1,)))


def mm_tn(left, right):
    return dot(left, right, ((0,), (0,)))


def to_peer(value, rel):
    if rel == 1:
        return lax.ppermute(value, "cols", [(0, 1), (1, 0)])
    if rel == 2:
        return lax.ppermute(value, "rows", [(0, 1), (1, 0)])
    return lax.ppermute(value, GROUP, [(i, i ^ 3) for i in range(4)])


def tie(values, others):
    flat, tree = jax.tree.flatten((values, others))
    return jax.tree.unflatten(tree, lax.optimization_barrier(flat))


def gather_tiles(value, others=()):
    across = to_peer(value, 2)
    beside = to_peer(value, 1)
    across, others = tie(across, others)
    return [value, beside, across, to_peer(across, 1)], others


def scatter_tiles(blocks):
    return [blocks[0], to_peer(blocks[1], 1), to_peer(blocks[2], 2), to_peer(blocks[3], 3)]


def norm_stats(values):
    mean_val = jnp.mean(values, axis=-1, keepdims=True)
    centred = values - mean_val
    var_val = jnp.mean(centred * centred, axis=-1, keepdims=True)
    inv = lax.rsqrt(var_val + NORM_EPS)
    return centred * inv, inv


def norm_back(grads, normed, inv, gain):
    g = grads * gain
    return (
        g
        - jnp.mean(g, axis=-1, keepdims=True)
        - normed * jnp.mean(g * normed, axis=-1, keepdims=True)
    ) * inv


def gelu_parts(x):
    cdf = 0.5 * (1.0 + lax.erf(x * 0.7071067811865476))
    pdf = jnp.exp(-0.5 * x * x) * 0.3989422804014327
    return x * cdf, cdf + x * pdf


def start_imgs(parts, imgs):
    if imgs % 2 or imgs > 8:
        return parts, None
    side = lax.axis_index("imgs") % 2
    split = parts.reshape((imgs // 2, 2) + parts.shape[1:])
    send = lax.dynamic_index_in_dim(split, 1 - side, 1, keepdims=False)
    keep = lax.dynamic_index_in_dim(split, side, 1, keepdims=False)
    return keep, lax.ppermute(send, "imgs", [(i, i ^ 1) for i in range(imgs)])


def finish_imgs(state, imgs, low):
    keep, got = state
    if got is None:
        return lax.psum_scatter(keep, "imgs", scatter_dimension=0, tiled=False).astype(F32)
    place = lax.axis_index("imgs") // 2
    line = imgs // 2

    def pick(index):
        at = jnp.clip(index, 0, line - 1)
        a = lax.dynamic_index_in_dim(keep, at, 0, keepdims=False)
        b = lax.dynamic_index_in_dim(got, at, 0, keepdims=False)
        return a.astype(F32) + b.astype(F32)

    def hop(value, step, up):
        pairs = []
        for z in range(line):
            for y in range(2):
                if up and z <= step - 1 and z + 1 < line:
                    pairs.append((2 * z + y, 2 * (z + 1) + y))
                if not up and z >= line - step and z - 1 >= 0:
                    pairs.append((2 * z + y, 2 * (z - 1) + y))
        return lax.ppermute(value.astype(low), "imgs", pairs).astype(F32)

    up_val = pick(place + line - 1)
    down_val = pick(place - (line - 1))
    for step in range(1, line):
        got_up = hop(up_val, step, True)
        got_down = hop(down_val, step, False)
        if step < line - 1:
            up_val = pick(place + line - 1 - step) + got_up
            down_val = pick(place - (line - 1) + step) + got_down
    return pick(place) + got_up + got_down


def own_order(blocks, tile):
    stacked = jnp.stack(blocks)
    return [lax.dynamic_index_in_dim(stacked, tile ^ k, 0, keepdims=False) for k in range(4)]


SMEM = pl.BlockSpec(memory_space=pltpu.SMEM)
VMEM = pl.BlockSpec(memory_space=pltpu.VMEM)
PAD = 16


def vec_call(kernel, outs, n_in, scratch=(), us=5):
    return pl.pallas_call(
        kernel,
        out_shape=outs,
        in_specs=[SMEM] + [VMEM] * n_in,
        out_specs=jax.tree.map(lambda _: VMEM, outs),
        scratch_shapes=list(scratch),
        cost_estimate=cost(us),
    )


def cost(us):
    return pl.CostEstimate(flops=us * 10**9, transcendentals=0, bytes_accessed=us * 10**6)


def sds(shape, dtype=BF):
    return jax.ShapeDtypeStruct(shape, dtype)


def load_tile(ref, scratch, at):
    rows, cols, width = ref.shape[1:]
    scratch[at : at + rows * PAD, :] = jnp.zeros((rows * PAD, width), scratch.dtype)
    for i in range(rows):
        scratch[at + i * PAD : at + i * PAD + cols, :] = ref[0, i]


def store_tile(ref, value):
    rows, cols, _ = ref.shape[1:]
    for i in range(rows):
        ref[0, i] = value[i * PAD : i * PAD + cols, :]


def mask_edges(mask):
    m = mask[0].astype(F32)
    high = jnp.sum(m[:, 0:1], axis=0, keepdims=True)
    wide = jnp.sum(m[0:1, :], axis=1, keepdims=True)
    return high, wide


def keep_tokens(edges, place, rows, cols, axis):
    toks = rows * PAD
    shape = (toks, 1) if axis == 0 else (1, toks)
    tok = lax.broadcasted_iota(jnp.int32, shape, axis)
    c = tok & (PAD - 1)
    r = ((tok >> 4) + (place >> 1) * rows).astype(F32)
    at = (c + (place & 1) * cols).astype(F32)
    ok = (c < cols) & (r < edges[0]) & (at < edges[1])
    return jnp.where(ok, 1.0, 0.0).astype(F32)


def vec_row(ref):
    return ref[...].reshape(1, -1)


def heads_kernel(tile, qkv_w, qv_b, w_own, b_own):
    width = qv_b.shape[1]
    part = width // 4
    for g in range(4):

        @pl.when(tile[0] == g)
        def _():
            for i in range(3):
                src = i * width + g * part
                w_own[:, i * part : (i + 1) * part] = qkv_w[:, src : src + part]
            b_own[:, :part] = qv_b[0:1, g * part : (g + 1) * part]
            b_own[:, part : 2 * part] = jnp.zeros((1, part), F32)
            b_own[:, 2 * part :] = qv_b[1:2, g * part : (g + 1) * part]


def units_kernel(tile, fc1, fc1_b, fc1_own, fc1_b_own, *, quarter):
    for g in range(4):

        @pl.when(tile[0] == g)
        def _():
            for i in range(fc1.shape[1] // (4 * quarter)):
                src = (4 * i + g) * quarter
                dst = i * quarter
                fc1_own[:, dst : dst + quarter] = fc1[:, src : src + quarter]
                fc1_b_own[:, dst : dst + quarter] = fc1_b[:, src : src + quarter]


def attn_kernel(
    tile, mask, x0, x1, x2, x3, gain, shift, w, bias, hid, nrm, qkv, lse, c0, c1, c2, c3, xs, ctx
):
    rows, cols, width = x0.shape[1:]
    toks = rows * PAD
    part = w.shape[1] // 3
    dim = width // HEADS
    scale = dim ** (-0.5)
    for r, ref in enumerate((x0, x1, x2, x3)):
        load_tile(ref, xs, r * toks)

    def project(r, carry):
        at = pl.ds(pl.multiple_of(r * toks, toks), toks)
        normed, _ = norm_stats(xs[at, :].astype(F32))
        h = (normed * vec_row(gain) + vec_row(shift)).astype(BF)
        hid[at, :] = h
        nrm[at, :] = normed.astype(BF)
        qkv[at, :] = (mm(h, w[...]) + bias[...]).astype(BF)
        return carry

    lax.fori_loop(0, 4, project, 0)
    edges = mask_edges(mask)
    keep = jnp.concatenate(
        [keep_tokens(edges, tile[0] ^ r, rows, cols, 1) for r in range(4)], axis=1
    )

    def attend(r, carry):
        at = pl.ds(pl.multiple_of(r * toks, toks), toks)
        outs = []
        for h in range(part // dim):
            q = qkv[at, h * dim : (h + 1) * dim]
            k = qkv[:, part + h * dim : part + (h + 1) * dim]
            v = qkv[:, 2 * part + h * dim : 2 * part + (h + 1) * dim]
            s = jnp.where(keep > 0, mm_nt(q * scale, k), MASKED_SCORE)
            top = jnp.max(s, axis=-1, keepdims=True)
            e = jnp.exp(s - top)
            total = jnp.sum(e, axis=-1, keepdims=True)
            outs.append(mm((e * (1.0 / total)).astype(BF), v).astype(BF))
            lse[at, h : h + 1] = top + jnp.log(total)
        ctx[r] = jnp.concatenate(outs, axis=1)
        return carry

    lax.fori_loop(0, 4, attend, 0)
    for r, ref in enumerate((c0, c1, c2, c3)):
        ref[...] = ctx[r]


def branch_kernel(tile, c0, c1, c2, c3, wo, bo, x, gain, shift, resid, hid, xs):
    part = c0.shape[1]
    load_tile(x, xs, 0)
    acc = xs[...].astype(F32) + vec_row(bo)
    for r, ref in enumerate((c0, c1, c2, c3)):
        at = pl.multiple_of((tile[0] ^ r) * part, part)
        acc = acc + mm(ref[...], wo[pl.ds(at, part), :])
    resid[...] = acc
    normed, _ = norm_stats(acc)
    hid[...] = (normed * vec_row(gain) + vec_row(shift)).astype(BF)


def mlp_kernel(
    tile, mask, resid, hid, ct, gain, fc1, fc1_b, fc2, fc2_b, out, branch, rgrad, vecs, up, acc, nacc
):
    step = pl.program_id(0)
    rows, cols, _ = ct.shape[1:]

    @pl.when(step == 0)
    def _():
        load_tile(ct, up, 0)
        up[...] = (up[...].astype(F32) * keep_tokens(mask_edges(mask), tile[0], rows, cols, 0)).astype(BF)
        acc[...] = jnp.zeros_like(acc)
        nacc[...] = jnp.zeros_like(nacc)

    act, dgelu = gelu_parts(mm(hid[...], fc1[...]) + fc1_b[...])
    acc[...] += mm(act.astype(BF), fc2[...])
    inner = (mm_nt(up[...], fc2[...]) * dgelu).astype(BF)
    nacc[...] += mm_nt(inner, fc1[...])

    @pl.when(step == pl.num_programs(0) - 1)
    def _():
        res = resid[...]
        keep = keep_tokens(mask_edges(mask), tile[0], rows, cols, 0)
        store_tile(out, (keep * (res + acc[...] + vec_row(fc2_b))).astype(BF))
        normed, inv = norm_stats(res)
        n = nacc[...]
        vecs[0:1, :] = jnp.sum(n * normed, axis=0, keepdims=True)
        vecs[1:2, :] = jnp.sum(n, axis=0, keepdims=True)
        grad = up[...].astype(F32) + norm_back(n, normed, inv, vec_row(gain))
        rgrad[...] = grad
        branch[...] = grad.astype(BF)


def ffgrad_kernel(
    tile, mask, h0, h1, h2, h3, t0, t1, t2, t3, fc1, fc1_b, fc2, g1, g2, b1, b2, up, a1, a2
):
    rows, cols, _ = t0.shape[1:]
    edges = mask_edges(mask)
    hids = (h0, h1, h2, h3)
    for r, ref in enumerate((t0, t1, t2, t3)):
        load_tile(ref, up, 0)
        wide = up[...].astype(F32) * keep_tokens(edges, tile[0] ^ r, rows, cols, 0)
        low = wide.astype(BF)
        h = hids[r][...]
        act, dgelu = gelu_parts(mm(h, fc1[...]) + fc1_b[...])
        inner = (mm_nt(low, fc2[...]) * dgelu).astype(BF)
        d1 = mm_tn(h, inner)
        d2 = mm_tn(act.astype(BF), low)
        s1 = jnp.sum(inner.astype(F32), axis=0, keepdims=True)
        s2 = jnp.sum(wide, axis=0, keepdims=True)
        if r == 0:
            a1[...], a2[...], b1[...], b2[...] = d1, d2, s1, s2
        elif r < 3:
            a1[...] += d1
            a2[...] += d2
            b1[...] += s1
            b2[...] += s2
        else:
            g1[...] = (a1[...] + d1).astype(BF)
            g2[...] = (a2[...] + d2).astype(BF)
            b1[...] += s1
            b2[...] += s2


def outgrad_kernel(tile, b0, b1, b2, b3, wo, c0, c1, c2, c3, dctx, gout, bsum):
    toks, part = c0.shape
    at = pl.multiple_of(tile[0] * part, part)
    w = wo[pl.ds(at, part), :]
    ctx = (c0, c1, c2, c3)
    acc = None
    total = None
    for r, ref in enumerate((b0, b1, b2, b3)):
        low = ref[...]
        dctx[r * toks : (r + 1) * toks, :] = mm_nt(low, w).astype(BF)
        d = mm_tn(ctx[r][...], low)
        s = jnp.sum(low.astype(F32), axis=0, keepdims=True)
        acc = d if r == 0 else acc + d
        total = s if r == 0 else total + s
    gout[...] = acc.astype(BF)
    bsum[...] = total


def attnback_kernel(
    tile, mask, dctx, qkv, lse, hid, nrm, w, m0, m1, m2, m3, gqkv, msum, nsum, dk, dv, mix, *, cols
):
    total, three = qkv.shape
    part = three // 3
    toks = total // 4
    dim = hid.shape[1] // HEADS
    rows = toks // PAD
    scale = dim ** (-0.5)
    edges = mask_edges(mask)
    keep = jnp.concatenate(
        [keep_tokens(edges, tile[0] ^ r, rows, cols, 1) for r in range(4)], axis=1
    )
    dk[...] = jnp.zeros_like(dk)
    dv[...] = jnp.zeros_like(dv)

    def attend(r, carry):
        at = pl.ds(pl.multiple_of(r * toks, toks), toks)
        dqs = []
        for h in range(part // dim):
            at_h = slice(h * dim, (h + 1) * dim)
            k = qkv[:, part + h * dim : part + (h + 1) * dim]
            v = qkv[:, 2 * part + h * dim : 2 * part + (h + 1) * dim]
            q = qkv[at, at_h] * scale
            do = dctx[at, at_h]
            s = jnp.where(keep > 0, mm_nt(q, k), MASKED_SCORE)
            p = jnp.exp(s - lse[at, h : h + 1])
            dp = mm_nt(do, v)
            ds = (p * (dp - jnp.sum(dp * p, axis=-1, keepdims=True))).astype(BF)
            dqs.append((mm(ds, k) * scale).astype(BF))
            dv[h] += mm_tn(p.astype(BF), do)
            dk[h] += mm_tn(ds, q)
        mix[at, :part] = jnp.concatenate(dqs, axis=1)
        return carry

    lax.fori_loop(0, 4, attend, 0)
    for h in range(part // dim):
        mix[:, part + h * dim : part + (h + 1) * dim] = dk[h].astype(BF)
        mix[:, 2 * part + h * dim : 2 * part + (h + 1) * dim] = dv[h].astype(BF)
    gqkv[...] = mm_tn(hid[...], mix[...]).astype(BF)
    for r, ref in enumerate((m0, m1, m2, m3)):
        at = slice(r * toks, (r + 1) * toks)
        m = mix[at, :]
        ref[...] = m
        n = mm_nt(m, w[...])
        a = jnp.sum(n * nrm[at, :].astype(F32), axis=0, keepdims=True)
        b = jnp.sum(n, axis=0, keepdims=True)
        c = jnp.sum(m.astype(F32), axis=0, keepdims=True)
        if r == 0:
            nsum[0:1, :] = a
            nsum[1:2, :] = b
            msum[...] = c
        else:
            nsum[0:1, :] += a
            nsum[1:2, :] += b
            msum[...] += c


def input_kernel(tile, m0, m1, m2, m3, w, x, rgrad, gain, out, ms, xs):
    part = m0.shape[1] // 3
    for r, ref in enumerate((m0, m1, m2, m3)):
        ms[r] = ref[...]
    tiles = [ms[tile[0] ^ g] for g in range(4)]
    full = jnp.concatenate(
        [m[:, i * part : (i + 1) * part] for i in range(3) for m in tiles], axis=1
    )
    n = mm_nt(full, w[...])
    load_tile(x, xs, 0)
    normed, inv = norm_stats(xs[...].astype(F32))
    store_tile(out, (rgrad[...] + norm_back(n, normed, inv, vec_row(gain))).astype(BF))


def ffout_kernel(tile, p0, p1, p2, p3, fc1, fc2, ps):
    rows = fc1.shape[0]
    quarter = fc2.shape[0] // 4
    for r, ref in enumerate((p0, p1, p2, p3)):
        ps[r] = ref[...].astype(F32)
    for g in range(4):
        piece = ps[tile[0] ^ g]
        for i in range(fc1.shape[1] // (4 * quarter)):
            dst = (4 * i + g) * quarter
            fc1[:, dst : dst + quarter] = piece[:rows, i * quarter : (i + 1) * quarter]
        fc2[g * quarter : (g + 1) * quarter, :] = piece[rows:, :]


def attnout_kernel(tile, p0, p1, p2, p3, gqkv, gout, vecs, ps):
    rows = gqkv.shape[0]
    width = gout.shape[1]
    part = width // 4
    for r, ref in enumerate((p0, p1, p2, p3)):
        ps[r] = ref[...].astype(F32)
    total = None
    for g in range(4):
        piece = ps[tile[0] ^ g]
        for i in range(3):
            dst = i * width + g * part
            gqkv[:, dst : dst + part] = piece[:rows, i * part : (i + 1) * part]
        gout[:, g * part : (g + 1) * part] = piece[:rows, 3 * part :]
        tail = piece[rows:, :]
        total = tail if g == 0 else total + tail
    vecs[...] = total


def body(
    patches,
    patch_mask,
    norm1_gain,
    norm1_shift,
    qkv_weight,
    qv_bias,
    out_weight,
    out_bias,
    norm2_gain,
    norm2_shift,
    fc1_weight,
    fc1_bias,
    fc2_weight,
    fc2_bias,
    cotangent,
):
    _, rows, cols, width = patches.shape
    ff = fc1_weight.shape[1]
    imgs = lax.axis_size("imgs")
    part = width // 4
    units = ff // 4
    quarter = units // imgs
    share = width // imgs
    toks = rows * PAD
    total = 4 * toks
    tile = lax.axis_index("rows") * 2 + lax.axis_index("cols")
    at_tile = tile.reshape(1).astype(jnp.int32)

    def row(v):
        return v.reshape(1, -1)

    steps = 4
    w_own, b_own = pl.pallas_call(
        heads_kernel,
        grid=(steps,),
        in_specs=[
            SMEM,
            pl.BlockSpec((width // steps, 3 * width), lambda i: (i, 0)),
            pl.BlockSpec((2, width), lambda i: (0, 0)),
        ],
        out_specs=[
            pl.BlockSpec((width // steps, 3 * part), lambda i: (i, 0)),
            pl.BlockSpec((1, 3 * part), lambda i: (0, 0)),
        ],
        out_shape=[sds((width, 3 * part)), sds((1, 3 * part), F32)],
        cost_estimate=cost(4),
        name="heads",
    )(at_tile, qkv_weight, qv_bias.T)
    x_blocks, (w_own, b_own) = gather_tiles(patches, (w_own, b_own))

    hid1, nrm1, qkv, lse, *ctx = vec_call(
        attn_kernel,
        [
            sds((total, width)),
            sds((total, width)),
            sds((total, 3 * part)),
            sds((total, 128), F32),
        ]
        + [sds((toks, part))] * 4,
        9,
        [pltpu.VMEM((total, width), BF), pltpu.VMEM((4, toks, part), BF)],
        us=13,
    )(at_tile, patch_mask, *x_blocks, norm1_gain, norm1_shift, w_own, b_own)
    ct_blocks, ctx = gather_tiles(cotangent, ctx)

    fc1_own, fc1_b_own = pl.pallas_call(
        functools.partial(units_kernel, quarter=quarter),
        grid=(steps,),
        in_specs=[
            SMEM,
            pl.BlockSpec((width // steps, ff), lambda i: (i, 0)),
            pl.BlockSpec((1, ff), lambda i: (0, 0)),
        ],
        out_specs=[
            pl.BlockSpec((width // steps, units), lambda i: (i, 0)),
            pl.BlockSpec((1, units), lambda i: (0, 0)),
        ],
        out_shape=[sds((width, units)), sds((1, units), F32)],
        cost_estimate=cost(4),
        name="units",
    )(at_tile, fc1_weight, row(fc1_bias))
    fc2_own = lax.dynamic_index_in_dim(
        fc2_weight.reshape(imgs, 4, quarter, width), tile, 1, keepdims=False
    ).reshape(units, width)

    ctx_in = scatter_tiles(ctx)
    ctx_in, (fc1_own, fc1_b_own, fc2_own) = tie(ctx_in, (fc1_own, fc1_b_own, fc2_own))
    resid, hid2 = vec_call(
        branch_kernel,
        [sds((toks, width), F32), sds((toks, width))],
        9,
        [pltpu.VMEM((toks, width), BF)],
        us=3,
    )(at_tile, *ctx_in, out_weight, out_bias, patches, norm2_gain, norm2_shift)

    chunks = 4
    step = ff // chunks

    def whole(*shape):
        return pl.BlockSpec(shape, lambda i: (0,) * len(shape))

    layer_out, branch, rgrad, vec2 = pl.pallas_call(
        mlp_kernel,
        grid=(chunks,),
        in_specs=[
            SMEM,
            whole(*patch_mask.shape),
            whole(toks, width),
            whole(toks, width),
            whole(1, rows, cols, width),
            whole(width),
            pl.BlockSpec((width, step), lambda i: (0, i)),
            pl.BlockSpec((1, step), lambda i: (0, i)),
            pl.BlockSpec((step, width), lambda i: (i, 0)),
            whole(width),
        ],
        out_specs=[
            whole(1, rows, cols, width),
            whole(toks, width),
            whole(toks, width),
            whole(2, width),
        ],
        out_shape=[
            sds((1, rows, cols, width)),
            sds((toks, width)),
            sds((toks, width), F32),
            sds((2, width), F32),
        ],
        scratch_shapes=[
            pltpu.VMEM((toks, width), BF),
            pltpu.VMEM((toks, width), F32),
            pltpu.VMEM((toks, width), F32),
        ],
        cost_estimate=cost(11),
        name="mlp",
    )(
        at_tile,
        patch_mask,
        resid,
        hid2,
        cotangent,
        norm2_gain,
        fc1_weight,
        row(fc1_bias),
        fc2_weight,
        fc2_bias,
    )
    hid2_blocks, (branch,) = gather_tiles(hid2, (branch,))

    g1, g2, fb1, fb2 = vec_call(
        ffgrad_kernel,
        [sds((width, units)), sds((units, width)), sds((1, units), F32), sds((1, width), F32)],
        12,
        [
            pltpu.VMEM((toks, width), BF),
            pltpu.VMEM((width, units), F32),
            pltpu.VMEM((units, width), F32),
        ],
        us=9,
    )(at_tile, patch_mask, *hid2_blocks, *ct_blocks, fc1_own, fc1_b_own, fc2_own)
    branch_blocks, (g1, g2) = gather_tiles(branch, (g1, g2))

    dctx, gout, bsum = vec_call(
        outgrad_kernel,
        [sds((total, part)), sds((part, width)), sds((1, width), F32)],
        9,
        us=4,
    )(at_tile, *branch_blocks, out_weight, *ctx)
    ff_bucket = jnp.concatenate(
        [g1.reshape(imgs, share, units), g2.reshape(imgs, quarter, width)], axis=1
    )
    ff_start = start_imgs(ff_bucket, imgs)
    out_cols = [lax.dynamic_slice_in_dim(gout, (tile ^ r) * part, part, 1) for r in range(4)]
    out_rows = scatter_tiles(out_cols)

    *mixed, gqkv, msum, nsum = vec_call(
        functools.partial(attnback_kernel, cols=cols),
        [sds((toks, 3 * part))] * 4
        + [
            sds((width, 3 * part)),
            sds((1, 3 * part), F32),
            sds((2, width), F32),
        ],
        7,
        [
            pltpu.VMEM((part * HEADS // width, total, width // HEADS), F32),
            pltpu.VMEM((part * HEADS // width, total, width // HEADS), F32),
            pltpu.VMEM((total, 3 * part), BF),
        ],
        us=18,
    )(at_tile, patch_mask, dctx, qkv, lse, hid1, nrm1, w_own)
    mixed_in = scatter_tiles(mixed)
    out_rows, (gqkv,) = tie(out_rows, (gqkv,))
    out_rows = own_order(out_rows, tile)

    lone = (tile == 0).astype(F32)
    fb1_row = lax.dynamic_update_index_in_dim(
        jnp.zeros((imgs, 4, quarter), F32), fb1.reshape(imgs, quarter), tile, 1
    )
    heads_row = lax.dynamic_update_index_in_dim(
        jnp.zeros((3, 4, part), F32), msum.reshape(3, part), tile, 1
    ).reshape(3, width)
    vec_rows = [nsum, heads_row, bsum * lone, vec2, fb2 * lone]
    vecs = jnp.concatenate(vec_rows, axis=0).reshape(9, imgs, share).transpose(1, 0, 2)
    vecs = jnp.concatenate(
        [vecs.reshape(imgs, 9 * share), fb1_row.reshape(imgs, 4 * quarter)], axis=1
    ).astype(BF)
    count = vecs.shape[1]
    vec_height = -(-count // width)
    vecs = jnp.pad(vecs, ((0, 0), (0, vec_height * width - count)))
    at_bucket = jnp.concatenate(
        [
            jnp.concatenate([gqkv, jnp.concatenate(out_rows, axis=0)], axis=1).reshape(
                imgs, share, width
            ),
            vecs.reshape(imgs, vec_height, width),
        ],
        axis=1,
    )
    at_start = start_imgs(at_bucket, imgs)
    ff_start, (mixed_in[0],) = tie(ff_start, (mixed_in[0],))
    ff_sum = finish_imgs(ff_start, imgs, BF)

    patches_grad = vec_call(
        input_kernel,
        sds((1, rows, cols, width)),
        8,
        [pltpu.VMEM((4, toks, 3 * part), BF), pltpu.VMEM((toks, width), BF)],
        us=5,
    )(at_tile, *mixed_in, qkv_weight, patches, rgrad, norm1_gain)

    at_start, (patches_grad, ff_sum) = tie(at_start, (patches_grad, ff_sum))
    ff_pieces, _ = gather_tiles(ff_sum.astype(BF))
    at_sum = finish_imgs(at_start, imgs, BF)
    fc1_grad, fc2_grad = vec_call(
        ffout_kernel,
        [sds((share, ff), F32), sds((4 * quarter, width), F32)],
        4,
        [pltpu.VMEM((4, share + quarter, width), F32)],
        us=3,
    )(at_tile, *ff_pieces)
    at_pieces, (fc1_grad, fc2_grad) = gather_tiles(at_sum.astype(BF), (fc1_grad, fc2_grad))
    qkv_grad, out_grad, vec_sum = vec_call(
        attnout_kernel,
        [sds((share, 3 * width), F32), sds((share, width), F32), sds((vec_height, width), F32)],
        4,
        [pltpu.VMEM((4, share + vec_height, width), F32)],
        us=3,
    )(at_tile, *at_pieces)
    v = vec_sum.reshape(-1)
    piece = [v[i * share : (i + 1) * share] for i in range(9)]
    return (
        layer_out,
        patches_grad,
        piece[0],
        piece[1],
        qkv_grad,
        jnp.stack([piece[2], piece[4]], axis=1),
        out_grad,
        piece[5],
        piece[6],
        piece[7],
        fc1_grad,
        v[9 * share : count],
        fc2_grad,
        piece[8],
    )


def solution(mesh):
    tiled = P("imgs", "rows", "cols", None)
    in_specs = (tiled, P("imgs", None, None)) + (P(),) * 12 + (tiled,)
    mat = P("imgs", None)
    vec = P("imgs")
    out_specs = (tiled, tiled, vec, vec, mat, mat, mat, vec, vec, vec, mat, vec, mat, vec)
    return jax.shard_map(body, mesh=mesh, in_specs=in_specs, out_specs=out_specs, check_vma=False)
```

profile of v0, /device:TPU:0, one launch (start us, length us, event | category | flops | bytes accessed | tf_op | source)
XLA Modules:
  0.0 191.9 jit_solution(3802544336752325983)
XLA Ops:
  0.6 3.0 %collective-permute-start.2 = (bf16[1,15,15,768]{3,2,1,0:T(8,128)(2,1)}, bf16[1,15,15,768]{3,2,1,0:T(8,128)(2,1)S(1)}, u32[]{:S(2)}, u32[]{:S(2)}) collective-permute-start(bf16[1,15,15,768]{3,2,1,0:T(8,128)(2,1)} %x.5), channel_id=1, source_target_pairs={{0,16},{16,0},{1,17},{17,1},{2,18},{18,2},{3,19},{19,3},{4,20},{20... | collective-permute-start | bytes 1036808 | tf_op jit(solution)/shard_map/ppermute | solution.py:38
  5.2 4.1 %heads.1 = (bf16[768,576]{1,0:T(8,128)(2,1)}, f32[1,576]{1,0:T(1,128)}) custom-call(s32[1]{0:T(128)} %bitcast.tile, bf16[768,2304]{1,0:T(8,128)(2,1)} %w.1, f32[2,768]{1,0:T(2,128)} %bitcast.106), custom_call_target="tpu_custom_call" | custom-call | flops 4000000000 | bytes 4000000 | tf_op jit(solution)/shard_map/heads/pallas_call | solution.py:492
  9.2 4.1 %collective-permute-done.2.x2 = bf16[1,15,15,768]{3,2,1,0:T(8,128)(2,1)S(1)} collective-permute-done((bf16[1,15,15,768]{3,2,1,0:T(8,128)(2,1)}, bf16[1,15,15,768]{3,2,1,0:T(8,128)(2,1)S(1)}, u32[]{:S(2)}, u32[]{:S(2)}) %collective-permute-start.2) | collective-permute-done | bytes 345632 | tf_op jit(solution)/shard_map/ppermute | solution.py:38
  13.3 4.7 %units.1 = (bf16[768,768]{1,0:T(8,128)(2,1)}, f32[1,768]{1,0:T(1,128)}) custom-call(s32[1]{0:T(128)} %bitcast.tile, bf16[768,3072]{1,0:T(8,128)(2,1)} %fc1.3, f32[1,3072]{1,0:T(1,128)} %bitcast.104), custom_call_target="tpu_custom_call" | custom-call | flops 4000000000 | bytes 4000000 | tf_op jit(solution)/shard_map/units/pallas_call | solution.py:525
  19.5 13.6 %shard_map.254 = (bf16[960,768]{1,0:T(8,128)(2,1)}, bf16[960,768]{1,0:T(8,128)(2,1)}, bf16[960,576]{1,0:T(8,128)(2,1)}, f32[960,128]{1,0:T(8,128)}, bf16[240,192...) custom-call(s32[1]{0:T(128)} %bitcast.tile, ...), custom_call_target="tpu_custom_call" | custom-call | flops 12999999488 | bytes 13000000 | tf_op jit(solution)/shard_map/pallas_call | solution.py:510
  35.5 2.4 %constant_dynamic-slice_fusion.4 = bf16[8,1,96,768]{3,2,1,0:T(8,128)(2,1)} fusion(bf16[8,4,96,768]{3,2,1,0:T(8,128)(2,1)} %bitcast.100, s32[]{:T(128)S(6)} %select_n.85), kind=kLoop, calls=%fused_computation.65 | loop fusion | bytes 2359300 | tf_op jit(solution)/shard_map/jit(dynamic_index_in_dim)/dynamic_slice | solution.py:541
  42.1 3.1 %shard_map.255 = (f32[240,768]{1,0:T(8,128)}, bf16[240,768]{1,0:T(8,128)(2,1)}) custom-call(s32[1]{0:T(128)} %bitcast.tile, bf16[240,192]{1,0:T(8,128)(2,1)} %get-tuple-element.101.c0, bf16[240,192]{1,0:T(8,128)(2,1)} %copy-done.26, bf16[240,192]{1,0:T(8,128)(2,1)} %copy-done.27, bf16[240,192]{1,0:T(8,128)(2,1)} %copy-done.28, bf16[768,768]{1,0:T(8,128)(2,1)} %wo.3, ...), custom_call_target="tpu_custom_call" | custom-call | flops 3000000000 | bytes 3000000 | tf_op jit(solution)/shard_map/pallas_call | solution.py:547
  47.1 10.5 %mlp.1 = (bf16[1,15,15,768]{3,2,1,0:T(8,128)(2,1)}, bf16[240,768]{1,0:T(8,128)(2,1)}, f32[240,768]{1,0:T(8,128)}, f32[2,768]{1,0:T(2,128)}) custom-call(s32[1]{0:T(128)} %bitcast.tile, s32[1,30,30]{2,1,0:T(8,128)} %copy.51.mask, f32[240,768]{1,0:T(8,128)} %get-tuple-element.105.resid, bf16[240,768]{1,0:T(8,128)(2,1)} %get-tuple-element.106.hid.h0, ...), custom_call_target="tpu_custom_call" | custom-call | flops 11000000512 | bytes 11000000 | tf_op jit(solution)/shard_map/mlp/pallas_call | solution.py:561
  62.1 9.1 %shard_map.256 = (bf16[768,768]{1,0:T(8,128)(2,1)}, bf16[768,768]{1,0:T(8,128)(2,1)}, f32[1,768]{1,0:T(1,128)}, f32[1,768]{1,0:T(1,128)}) custom-call(s32[1]{0:T(128)} %bitcast.tile, s32[1,30,30]{2,1,0:T(8,128)} %copy.51.mask, bf16[240,768]{1,0:T(8,128)(2,1)} %get-tuple-element.106.hid.h0, bf16[240,768]{1,0:T(8,128)(2,1)} %copy-done.15, ...), custom_call_target="tpu_custom_call" | custom-call | flops 8999999488 | bytes 9000000 | tf_op jit(solution)/shard_map/pallas_call | solution.py:609
  71.5 2.8 %fusion.1 = (bf16[4,192,768]{2,1,0:T(8,128)(2,1)}, bf16[4,192,768]{2,1,0:T(8,128)(2,1)S(1)}) fusion(s32[]{:T(128)S(6)} %select_n.95, bf16[4,2,96,768]{3,2,1,0:T(8,128)(2,1)} %bitcast.96, bf16[4,2,96,768]{3,2,1,0:T(8,128)(2,1)} %bitcast.97, s32[]{:T(128)S(6)} %select_n.94), kind=kLoop, calls=%fused_computation.7 | loop fusion | flops 4718592 | bytes 4718600 | tf_op jit(solution)/shard_map/jit(dynamic_index_in_dim)/squeeze | solution.py:86
  76.9 3.5 %shard_map.257 = (bf16[960,192]{1,0:T(8,128)(2,1)}, bf16[192,768]{1,0:T(8,128)(2,1)}, f32[1,768]{1,0:T(1,128)}) custom-call(s32[1]{0:T(128)} %bitcast.tile, bf16[240,768]{1,0:T(8,128)(2,1)} %get-tuple-element.109.b0, bf16[240,768]{1,0:T(8,128)(2,1)} %copy-done.10, bf16[240,768]{1,0:T(8,128)(2,1)} %copy-done.9, bf16[240,768]{1,0:T(8,128)(2,1)} %collective-permute-done.14.b3, ...), custom_call_target="tpu_custom_call" | custom-call | flops 4000000000 | bytes 4000000 | tf_op jit(solution)/shard_map/pallas_call | solution.py:622
  80.4 19.1 %shard_map.258 = (bf16[240,576]{1,0:T(8,128)(2,1)}, bf16[240,576]{1,0:T(8,128)(2,1)}, bf16[240,576]{1,0:T(8,128)(2,1)}, bf16[240,576]{1,0:T(8,128)(2,1)}, bf16[7...) custom-call(s32[1]{0:T(128)} %bitcast.tile, s32[1,30,30]{2,1,0:T(8,128)} %copy.51.mask, ...), custom_call_target="tpu_custom_call" | custom-call | flops 17999998976 | bytes 18000000 | tf_op jit(solution)/shard_map/pallas_call | solution.py:635
  102.8 4.2 %collective-permute-start.23 = (bf16[192,768]{1,0:T(8,128)(2,1)S(1)}, bf16[192,768]{1,0:T(8,128)(2,1)}, u32[]{:S(2)}, u32[]{:S(2)}) collective-permute-start(bf16[192,768]{1,0:T(8,128)(2,1)S(1)} %get-tuple-element.160), channel_id=1, source_target_pairs={{0,2},{1,3},{8,10},{9,11},{16,18},{17,19},{24,26},{25,27}} | collective-permute-start | bytes 884744 | tf_op jit(solution)/shard_map/ppermute | solution.py:112
  113.3 5.2 %collective-permute-start.24 = (bf16[192,768]{1,0:T(8,128)(2,1)S(1)}, bf16[192,768]{1,0:T(8,128)(2,1)}, u32[]{:S(2)}, u32[]{:S(2)}) collective-permute-start(bf16[192,768]{1,0:T(8,128)(2,1)S(1)} %fusion.10), channel_id=1, source_target_pairs={{0,2},{1,3},{2,4},{3,5},{8,10},{9,11},{10,12},{11,13},{16,18},{17,... | collective-permute-start | bytes 884744 | tf_op jit(solution)/shard_map/ppermute | solution.py:112
  127.7 10.2 %collective-permute-start.25 = (bf16[192,768]{1,0:T(8,128)(2,1)S(1)}, bf16[192,768]{1,0:T(8,128)(2,1)}, u32[]{:S(2)}, u32[]{:S(2)}) collective-permute-start(bf16[192,768]{1,0:T(8,128)(2,1)S(1)} %get-tuple-element.158), channel_id=1, source_target_pairs={{0,2},{1,3},{2,4},{3,5},{4,6},{5,7},{8,10},{9,11},{10,12},{11,13},... | collective-permute-start | bytes 884744 | tf_op jit(solution)/shard_map/ppermute | solution.py:112
  140.0 4.9 %shard_map.259 = bf16[1,15,15,768]{3,2,1,0:T(8,128)(2,1)} custom-call(s32[1]{0:T(128)} %bitcast.tile, bf16[240,576]{1,0:T(8,128)(2,1)} %get-tuple-element.139.m0, bf16[240,576]{1,0:T(8,128)(2,1)} %collective-permute-done.20.m1, bf16[240,576]{1,0:T(8,128)(2,1)} %collective-permute-done.21.m2, bf16[240,576]{1,0:T(8,128)(2,1)} %collective-permute-done.22.m3, ...), custom_call_target="tpu_custom_call" | custom-call | flops 5000000000 | bytes 5000000 | tf_op jit(solution)/shard_map/pallas_call | solution.py:683
  145.0 2.7 %collective-permute-done.28 = bf16[192,768]{1,0:T(8,128)(2,1)} collective-permute-done((bf16[192,768]{1,0:T(8,128)(2,1)}, bf16[192,768]{1,0:T(8,128)(2,1)}, u32[]{:S(2)}, u32[]{:S(2)}) %collective-permute-start.28) | collective-permute-done | bytes 294944 | tf_op jit(solution)/shard_map/ppermute | solution.py:112
  152.8 2.2 %collective-permute-done.29 = bf16[98,768]{1,0:T(8,128)(2,1)S(1)} collective-permute-done((bf16[98,768]{1,0:T(8,128)(2,1)S(1)}, bf16[98,768]{1,0:T(8,128)(2,1)S(1)}, u32[]{:S(2)}, u32[]{:S(2)}) %collective-permute-start.29) | collective-permute-done | bytes 150560 | tf_op jit(solution)/shard_map/ppermute | solution.py:112
  155.0 4.4 %collective-permute-start.30 = (bf16[98,768]{1,0:T(8,128)(2,1)S(1)}, bf16[98,768]{1,0:T(8,128)(2,1)S(1)}, u32[]{:S(2)}, u32[]{:S(2)}) collective-permute-start(bf16[98,768]{1,0:T(8,128)(2,1)S(1)} %fusion.15), channel_id=1, source_target_pairs={{0,2},{1,3},{2,4},{3,5},{8,10},{9,11},{10,12},{11,13},{16,18},{17,... | collective-permute-start | bytes 451592 | tf_op jit(solution)/shard_map/ppermute | solution.py:112
  159.5 2.8 %collective-permute-done.30 = bf16[98,768]{1,0:T(8,128)(2,1)S(1)} collective-permute-done((bf16[98,768]{1,0:T(8,128)(2,1)S(1)}, bf16[98,768]{1,0:T(8,128)(2,1)S(1)}, u32[]{:S(2)}, u32[]{:S(2)}) %collective-permute-start.30) | collective-permute-done | bytes 150560 | tf_op jit(solution)/shard_map/ppermute | solution.py:112
  163.6 5.0 %collective-permute-start.31 = (bf16[98,768]{1,0:T(8,128)(2,1)S(1)}, bf16[98,768]{1,0:T(8,128)(2,1)S(1)}, u32[]{:S(2)}, u32[]{:S(2)}) collective-permute-start(bf16[98,768]{1,0:T(8,128)(2,1)S(1)} %get-tuple-element.164), channel_id=1, source_target_pairs={{0,2},{1,3},{2,4},{3,5},{4,6},{5,7},{8,10},{9,11},{10,12},{11,13},... | collective-permute-start | bytes 451592 | tf_op jit(solution)/shard_map/ppermute | solution.py:112
  171.4 6.8 %collective-permute-done.34 = bf16[98,768]{1,0:T(8,128)(2,1)S(1)} collective-permute-done((bf16[98,768]{1,0:T(8,128)(2,1)S(1)}, bf16[98,768]{1,0:T(8,128)(2,1)S(1)}, u32[]{:S(2)}, u32[]{:S(2)}) %collective-permute-start.34) | collective-permute-done | bytes 150560 | tf_op jit(solution)/shard_map/ppermute | solution.py:112
  180.9 3.3 %shard_map.260 = (f32[96,3072]{1,0:T(8,128)}, f32[384,768]{1,0:T(8,128)}) custom-call(s32[1]{0:T(128)} %bitcast.tile, bf16[192,768]{1,0:T(8,128)(2,1)} %copy-done.2, bf16[192,768]{1,0:T(8,128)(2,1)} %copy-done.21, bf16[192,768]{1,0:T(8,128)(2,1)} %copy-done.20, bf16[192,768]{1,0:T(8,128)(2,1)} %copy-done.22), custom_call_target="tpu_custom_call" | custom-call | flops 3000000000 | bytes 3000000 | tf_op jit(solution)/shard_map/pallas_call | solution.py:694
  186.9 2.5 %shard_map.261 = (f32[96,2304]{1,0:T(8,128)}, f32[96,768]{1,0:T(8,128)}, f32[2,768]{1,0:T(2,128)}) custom-call(s32[1]{0:T(128)} %bitcast.tile, bf16[98,768]{1,0:T(8,128)(2,1)} %copy-done.3, bf16[98,768]{1,0:T(8,128)(2,1)} %copy-done.24, bf16[98,768]{1,0:T(8,128)(2,1)} %copy-done.23, bf16[98,768]{1,0:T(8,128)(2,1)} %copy-done.25), custom_call_target="tpu_custom_call" | custom-call | flops 3000000000 | bytes 3000000 | tf_op jit(solution)/shard_map/pallas_call | solution.py:702
  (178 shorter events, 56.7 us)
Async XLA Ops:
  0.6 12.7 %collective-permute-start.2 = (bf16[1,15,15,768]{3,2,1,0:T(8,128)(2,1)}, bf16[1,15,15,768]{3,2,1,0:T(8,128)(2,1)S(1)}, u32[]{:S(2)}, u32[]{:S(2)}) collective-permute-start(bf16[1,15,15,768]{3,2,1,0:T(8,128)(2,1)} %x.5), channel_id=1, source_target_pairs={{0,16},{16,0},{1,17},{17,1},{2,18},{18,2},{3,19},{19,3},{4,20},{20... | collective-permute-start | bytes 1036808 | tf_op jit(solution)/shard_map/ppermute | solution.py:38
  3.7 14.3 %collective-permute-start.1 = (bf16[1,15,15,768]{3,2,1,0:T(8,128)(2,1)}, bf16[1,15,15,768]{3,2,1,0:T(8,128)(2,1)S(1)}, u32[]{:S(2)}, u32[]{:S(2)}) collective-permute-start(bf16[1,15,15,768]{3,2,1,0:T(8,128)(2,1)} %x.5), channel_id=1, source_target_pairs={{0,8},{8,0},{1,9},{9,1},{2,10},{10,2},{3,11},{11,3},{4,12},{12,4},... | collective-permute-start | bytes 1036808 | tf_op jit(solution)/shard_map/ppermute | solution.py:36
  3.7 29.4 %collective-permute-start = (bf16[1,15,15,768]{3,2,1,0:T(8,128)(2,1)}, bf16[1,15,15,768]{3,2,1,0:T(8,128)(2,1)S(1)}, u32[]{:S(2)}, u32[]{:S(2)}) collective-permute-start(bf16[1,15,15,768]{3,2,1,0:T(8,128)(2,1)} %t0.1), channel_id=1, source_target_pairs={{0,16},{16,0},{1,17},{17,1},{2,18},{18,2},{3,19},{19,3},{4,20},{20... | collective-permute-start | bytes 1036808 | tf_op jit(solution)/shard_map/ppermute | solution.py:38
  45.2 12.4 %collective-permute-start.7 = (bf16[240,768]{1,0:T(8,128)(2,1)}, bf16[240,768]{1,0:T(8,128)(2,1)S(1)}, u32[]{:S(2)}, u32[]{:S(2)}) collective-permute-start(bf16[240,768]{1,0:T(8,128)(2,1)} %get-tuple-element.106.hid.h0), channel_id=1, source_target_pairs={{0,16},{16,0},{1,17},{17,1},{2,18},{18,2},{3,19},{19,3},{4,20},{20... | collective-permute-start | bytes 1105928 | tf_op jit(solution)/shard_map/ppermute | solution.py:38
  46.7 13.7 %collective-permute-start.10 = (bf16[240,768]{1,0:T(8,128)(2,1)}, bf16[240,768]{1,0:T(8,128)(2,1)S(1)}, u32[]{:S(2)}, u32[]{:S(2)}) collective-permute-start(bf16[240,768]{1,0:T(8,128)(2,1)} %get-tuple-element.106.hid.h0), channel_id=1, source_target_pairs={{0,8},{8,0},{1,9},{9,1},{2,10},{10,2},{3,11},{11,3},{4,12},{12,4},... | collective-permute-start | bytes 1105928 | tf_op jit(solution)/shard_map/ppermute | solution.py:36
  58.4 12.8 %collective-permute-start.9 = (bf16[240,768]{1,0:T(8,128)(2,1)}, bf16[240,768]{1,0:T(8,128)(2,1)S(1)}, u32[]{:S(2)}, u32[]{:S(2)}) collective-permute-start(bf16[240,768]{1,0:T(8,128)(2,1)} %get-tuple-element.109.b0), channel_id=1, source_target_pairs={{0,16},{16,0},{1,17},{17,1},{2,18},{18,2},{3,19},{19,3},{4,20},{20... | collective-permute-start | bytes 1105928 | tf_op jit(solution)/shard_map/ppermute | solution.py:38
  59.9 16.2 %collective-permute-start.8 = (bf16[240,768]{1,0:T(8,128)(2,1)}, bf16[240,768]{1,0:T(8,128)(2,1)S(1)}, u32[]{:S(2)}, u32[]{:S(2)}) collective-permute-start(bf16[240,768]{1,0:T(8,128)(2,1)} %get-tuple-element.109.b0), channel_id=1, source_target_pairs={{0,8},{8,0},{1,9},{9,1},{2,10},{10,2},{3,11},{11,3},{4,12},{12,4},... | collective-permute-start | bytes 1105928 | tf_op jit(solution)/shard_map/ppermute | solution.py:36
  74.3 28.5 %collective-permute-start.19 = (bf16[4,192,768]{2,1,0:T(8,128)(2,1)}, bf16[4,192,768]{2,1,0:T(8,128)(2,1)S(1)}, u32[]{:S(2)}, u32[]{:S(2)}) collective-permute-start(bf16[4,192,768]{2,1,0:T(8,128)(2,1)} %get-tuple-element.162), channel_id=1, source_target_pairs={{0,1},{1,0},{2,3},{3,2},{4,5},{5,4},{6,7},{7,6},{8,9},{9,8},{10,11... | collective-permute-start | bytes 3538952 | tf_op jit(solution)/shard_map/ppermute | solution.py:88
  102.8 9.4 %collective-permute-start.23 = (bf16[192,768]{1,0:T(8,128)(2,1)S(1)}, bf16[192,768]{1,0:T(8,128)(2,1)}, u32[]{:S(2)}, u32[]{:S(2)}) collective-permute-start(bf16[192,768]{1,0:T(8,128)(2,1)S(1)} %get-tuple-element.160), channel_id=1, source_target_pairs={{0,2},{1,3},{8,10},{9,11},{16,18},{17,19},{24,26},{25,27}} | collective-permute-start | bytes 884744 | tf_op jit(solution)/shard_map/ppermute | solution.py:112
  108.1 10.6 %collective-permute-start.15 = (bf16[192,192]{1,0:T(8,128)(2,1)}, bf16[192,192]{1,0:T(8,128)(2,1)S(1)}, u32[]{:S(2)}, u32[]{:S(2)}) collective-permute-start(bf16[192,192]{1,0:T(8,128)(2,1)} %get-tuple-element.176), channel_id=1, source_target_pairs={{0,8},{8,0},{1,9},{9,1},{2,10},{10,2},{3,11},{11,3},{4,12},{12,4},... | collective-permute-start | bytes 221192 | tf_op jit(solution)/shard_map/ppermute | solution.py:36
  108.1 10.7 %collective-permute-start.16 = (bf16[192,192]{1,0:T(8,128)(2,1)}, bf16[192,192]{1,0:T(8,128)(2,1)}, u32[]{:S(2)}, u32[]{:S(2)}) collective-permute-start(bf16[192,192]{1,0:T(8,128)(2,1)} %get-tuple-element.175), channel_id=1, source_target_pairs={{0,16},{16,0},{1,17},{17,1},{2,18},{18,2},{3,19},{19,3},{4,20},{20... | collective-permute-start | bytes 221192 | tf_op jit(solution)/shard_map/ppermute | solution.py:38
  108.6 10.7 %collective-permute-start.17 = (bf16[192,192]{1,0:T(8,128)(2,1)}, bf16[192,192]{1,0:T(8,128)(2,1)}, u32[]{:S(2)}, u32[]{:S(2)}) collective-permute-start(bf16[192,192]{1,0:T(8,128)(2,1)} %get-tuple-element.174), channel_id=1, source_target_pairs={{0,24},{8,16},{16,8},{24,0},{1,25},{9,17},{17,9},{25,1},{2,26},{10... | collective-permute-start | bytes 221192 | tf_op jit(solution)/shard_map/ppermute | solution.py:39
  109.9 11.7 %collective-permute-start.26 = (bf16[192,768]{1,0:T(8,128)(2,1)S(1)}, bf16[192,768]{1,0:T(8,128)(2,1)S(1)}, u32[]{:S(2)}, u32[]{:S(2)}) collective-permute-start(bf16[192,768]{1,0:T(8,128)(2,1)S(1)} %get-tuple-element.161), channel_id=1, source_target_pairs={{6,4},{7,5},{14,12},{15,13},{22,20},{23,21},{30,28},{31,29}} | collective-permute-start | bytes 884744 | tf_op jit(solution)/shard_map/ppermute | solution.py:112
  113.3 9.6 %collective-permute-start.24 = (bf16[192,768]{1,0:T(8,128)(2,1)S(1)}, bf16[192,768]{1,0:T(8,128)(2,1)}, u32[]{:S(2)}, u32[]{:S(2)}) collective-permute-start(bf16[192,768]{1,0:T(8,128)(2,1)S(1)} %fusion.10), channel_id=1, source_target_pairs={{0,2},{1,3},{2,4},{3,5},{8,10},{9,11},{10,12},{11,13},{16,18},{17,... | collective-permute-start | bytes 884744 | tf_op jit(solution)/shard_map/ppermute | solution.py:112
  118.7 20.1 %collective-permute-start.20 = (bf16[240,576]{1,0:T(8,128)(2,1)}, bf16[240,576]{1,0:T(8,128)(2,1)}, u32[]{:S(2)}, u32[]{:S(2)}) collective-permute-start(bf16[240,576]{1,0:T(8,128)(2,1)} %get-tuple-element.140), channel_id=1, source_target_pairs={{0,8},{8,0},{1,9},{9,1},{2,10},{10,2},{3,11},{11,3},{4,12},{12,4},... | collective-permute-start | bytes 829448 | tf_op jit(solution)/shard_map/ppermute | solution.py:36
  118.7 21.3 %collective-permute-start.21 = (bf16[240,576]{1,0:T(8,128)(2,1)}, bf16[240,576]{1,0:T(8,128)(2,1)}, u32[]{:S(2)}, u32[]{:S(2)}) collective-permute-start(bf16[240,576]{1,0:T(8,128)(2,1)} %get-tuple-element.141), channel_id=1, source_target_pairs={{0,16},{16,0},{1,17},{17,1},{2,18},{18,2},{3,19},{19,3},{4,20},{20... | collective-permute-start | bytes 829448 | tf_op jit(solution)/shard_map/ppermute | solution.py:38
  119.4 20.7 %collective-permute-start.22 = (bf16[240,576]{1,0:T(8,128)(2,1)}, bf16[240,576]{1,0:T(8,128)(2,1)}, u32[]{:S(2)}, u32[]{:S(2)}) collective-permute-start(bf16[240,576]{1,0:T(8,128)(2,1)} %get-tuple-element.142), channel_id=1, source_target_pairs={{0,24},{8,16},{16,8},{24,0},{1,25},{9,17},{17,9},{25,1},{2,26},{10... | collective-permute-start | bytes 829448 | tf_op jit(solution)/shard_map/ppermute | solution.py:39
  126.2 22.7 %collective-permute-start.18 = (bf16[4,98,768]{2,0,1:T(4,128)(2,1)}, bf16[4,98,768]{2,0,1:T(4,128)(2,1)}, u32[]{:S(2)}, u32[]{:S(2)}) collective-permute-start(bf16[4,98,768]{2,0,1:T(4,128)(2,1)} %bitcast.94), channel_id=1, source_target_pairs={{0,1},{1,0},{2,3},{3,2},{4,5},{5,4},{6,7},{7,6},{8,9},{9,8},{10,11... | collective-permute-start | bytes 1806344 | tf_op jit(solution)/shard_map/ppermute | solution.py:88
  127.7 17.2 %collective-permute-start.25 = (bf16[192,768]{1,0:T(8,128)(2,1)S(1)}, bf16[192,768]{1,0:T(8,128)(2,1)}, u32[]{:S(2)}, u32[]{:S(2)}) collective-permute-start(bf16[192,768]{1,0:T(8,128)(2,1)S(1)} %get-tuple-element.158), channel_id=1, source_target_pairs={{0,2},{1,3},{2,4},{3,5},{4,6},{5,7},{8,10},{9,11},{10,12},{11,13},... | collective-permute-start | bytes 884744 | tf_op jit(solution)/shard_map/ppermute | solution.py:112
  138.7 8.9 %collective-permute-start.28 = (bf16[192,768]{1,0:T(8,128)(2,1)}, bf16[192,768]{1,0:T(8,128)(2,1)}, u32[]{:S(2)}, u32[]{:S(2)}) collective-permute-start(bf16[192,768]{1,0:T(8,128)(2,1)} %fusion.9), channel_id=1, source_target_pairs={{2,0},{3,1},{4,2},{5,3},{6,4},{7,5},{10,8},{11,9},{12,10},{13,11},... | collective-permute-start | bytes 884744 | tf_op jit(solution)/shard_map/ppermute | solution.py:112
  163.6 7.8 %collective-permute-start.31 = (bf16[98,768]{1,0:T(8,128)(2,1)S(1)}, bf16[98,768]{1,0:T(8,128)(2,1)S(1)}, u32[]{:S(2)}, u32[]{:S(2)}) collective-permute-start(bf16[98,768]{1,0:T(8,128)(2,1)S(1)} %get-tuple-element.164), channel_id=1, source_target_pairs={{0,2},{1,3},{2,4},{3,5},{4,6},{5,7},{8,10},{9,11},{10,12},{11,13},... | collective-permute-start | bytes 451592 | tf_op jit(solution)/shard_map/ppermute | solution.py:112
  168.7 9.5 %collective-permute-start.34 = (bf16[98,768]{1,0:T(8,128)(2,1)S(1)}, bf16[98,768]{1,0:T(8,128)(2,1)S(1)}, u32[]{:S(2)}, u32[]{:S(2)}) collective-permute-start(bf16[98,768]{1,0:T(8,128)(2,1)S(1)} %fusion.14), channel_id=1, source_target_pairs={{2,0},{3,1},{4,2},{5,3},{6,4},{7,5},{10,8},{11,9},{12,10},{13,11},... | collective-permute-start | bytes 451592 | tf_op jit(solution)/shard_map/ppermute | solution.py:112
  170.0 9.5 %collective-permute-start.37 = (bf16[192,768]{1,0:T(8,128)(2,1)S(1)}, bf16[192,768]{1,0:T(8,128)(2,1)S(1)}, u32[]{:S(2)}, u32[]{:S(2)}) collective-permute-start(bf16[192,768]{1,0:T(8,128)(2,1)S(1)} %fusion.12.p0), channel_id=1, source_target_pairs={{0,8},{8,0},{1,9},{9,1},{2,10},{10,2},{3,11},{11,3},{4,12},{12,4},... | collective-permute-start | bytes 884744 | tf_op jit(solution)/shard_map/ppermute | solution.py:36
  170.1 9.4 %collective-permute-start.39 = (bf16[192,768]{1,0:T(8,128)(2,1)S(1)}, bf16[192,768]{1,0:T(8,128)(2,1)S(1)}, u32[]{:S(2)}, u32[]{:S(2)}) collective-permute-start(bf16[192,768]{1,0:T(8,128)(2,1)S(1)} %collective-permute-done.38.p2), channel_id=1, source_target_pairs={{0,8},{8,0},{1,9},{9,1},{2,10},{10,2},{3,11},{11,3},{4,12},{12,4},... | collective-permute-start | bytes 884744 | tf_op jit(solution)/shard_map/ppermute | solution.py:36
  (46 other events, 231.7 us)
where the time goes:
time: 193 us; the launch traced here: 192 us
  Pallas kernels  78.4 us (41%)
  starting transfers between devices  54.8 us (28%)
  waiting for transfers between devices  29.7 us (15%)
  local copies, waits for them, and re-layouts  16.8 us (9%)
  other arithmetic  11.1 us (6%)
    ppermute x12, starting transfers between devices, hop(): return lax.ppermute(value.astype(low), 'imgs', pairs).astype(F32)  36.1 us
    pallas_call x1, Pallas kernels, body(): vec_call(functools.partial(attnback_kernel, cols=cols), [sds((toks, 3 * p...  19.1 us
    ppermute x12, waiting for transfers between devices, hop(): return lax.ppermute(value.astype(low), 'imgs', pairs).astype(F32)  18.2 us
    pallas_call x1, Pallas kernels, body(): vec_call(attn_kernel, [sds((total, width)), sds((total, width)), sds((tot...  13.6 us
    pallas_call x1, Pallas kernels, body(): pl.pallas_call(mlp_kernel, grid=(chunks,), in_specs=[SMEM, whole(*patch_m...  10.5 us
    ppermute x9, starting transfers between devices, to_peer(): return lax.ppermute(value, 'rows', [(0, 1), (1, 0)])  10.1 us
    pallas_call x1, Pallas kernels, body(): vec_call(ffgrad_kernel, [sds((width, units)), sds((units, width)), sds((1...  9.07 us
    unnamed x63, local copies, waits for them, and re-layouts  8.33 us
  transfers between devices with their start and end apart: 41, of which 15 were waited for; matrix products, arithmetic and copies ran while one was open for 9% of the time, Pallas kernels for 38%

commit v1 on v0

--- a/solution.py
+++ b/solution.py
@@ -78,48 +78,34 @@
     return x * cdf, cdf + x * pdf
 
 
-def start_imgs(parts, imgs):
-    if imgs % 2 or imgs > 8:
-        return parts, None
+def exchange_near(parts):
     side = lax.axis_index("imgs") % 2
-    split = parts.reshape((imgs // 2, 2) + parts.shape[1:])
-    send = lax.dynamic_index_in_dim(split, 1 - side, 1, keepdims=False)
-    keep = lax.dynamic_index_in_dim(split, side, 1, keepdims=False)
-    return keep, lax.ppermute(send, "imgs", [(i, i ^ 1) for i in range(imgs)])
-
-
-def finish_imgs(state, imgs, low):
-    keep, got = state
-    if got is None:
-        return lax.psum_scatter(keep, "imgs", scatter_dimension=0, tiled=False).astype(F32)
+    count = lax.axis_size("imgs")
+    send = lax.dynamic_index_in_dim(parts, 1 - side, 1, keepdims=False)
+    keep = lax.dynamic_index_in_dim(parts, side, 1, keepdims=False)
+    return keep, lax.ppermute(send, "imgs", [(i, i ^ 1) for i in range(count)])
+
+
+def exchange_far(parts):
+    count = lax.axis_size("imgs")
     place = lax.axis_index("imgs") // 2
-    line = imgs // 2
-
-    def pick(index):
-        at = jnp.clip(index, 0, line - 1)
-        a = lax.dynamic_index_in_dim(keep, at, 0, keepdims=False)
-        b = lax.dynamic_index_in_dim(got, at, 0, keepdims=False)
-        return a.astype(F32) + b.astype(F32)
-
-    def hop(value, step, up):
-        pairs = []
-        for z in range(line):
-            for y in range(2):
-                if up and z <= step - 1 and z + 1 < line:
-                    pairs.append((2 * z + y, 2 * (z + 1) + y))
-                if not up and z >= line - step and z - 1 >= 0:
-                    pairs.append((2 * z + y, 2 * (z - 1) + y))
-        return lax.ppermute(value.astype(low), "imgs", pairs).astype(F32)
-
-    up_val = pick(place + line - 1)
-    down_val = pick(place - (line - 1))
-    for step in range(1, line):
-        got_up = hop(up_val, step, True)
-        got_down = hop(down_val, step, False)
-        if step < line - 1:
-            up_val = pick(place + line - 1 - step) + got_up
-            down_val = pick(place - (line - 1) + step) + got_down
-    return pick(place) + got_up + got_down
+    got = [lax.dynamic_index_in_dim(parts, place, 0, keepdims=False)]
+    for k in range(count // 2 - 1, 0, -1):
+        send = lax.dynamic_index_in_dim(parts, place ^ k, 0, keepdims=False)
+        got.append(lax.ppermute(send, "imgs", [(i, i ^ (2 * k)) for i in range(count)]))
+    return got
+
+
+def total_of(blocks):
+    return functools.reduce(jnp.add, [b.astype(F32) for b in blocks])
+
+
+def direct_sum(imgs):
+    return imgs <= 8 and imgs & (imgs - 1) == 0
+
+
+def plain_sum(parts):
+    return lax.psum_scatter(parts, "imgs", scatter_dimension=0, tiled=False)
 
 
 def own_order(blocks, tile):
@@ -354,7 +340,28 @@
 
 
 def attnback_kernel(
-    tile, mask, dctx, qkv, lse, hid, nrm, w, m0, m1, m2, m3, gqkv, msum, nsum, dk, dv, mix, *, cols
+    tile,
+    mask,
+    dctx,
+    qkv,
+    lse,
+    hid,
+    nrm,
+    w,
+    bsum,
+    vec2,
+    fb2,
+    m0,
+    m1,
+    m2,
+    m3,
+    gqkv,
+    vecs,
+    dk,
+    dv,
+    mix,
+    *,
+    cols,
 ):
     total, three = qkv.shape
     part = three // 3
@@ -401,14 +408,19 @@
         a = jnp.sum(n * nrm[at, :].astype(F32), axis=0, keepdims=True)
         b = jnp.sum(n, axis=0, keepdims=True)
         c = jnp.sum(m.astype(F32), axis=0, keepdims=True)
-        if r == 0:
-            nsum[0:1, :] = a
-            nsum[1:2, :] = b
-            msum[...] = c
-        else:
-            nsum[0:1, :] += a
-            nsum[1:2, :] += b
-            msum[...] += c
+        sums = (a, b, c) if r == 0 else tuple(s + t for s, t in zip(sums, (a, b, c)))
+    gain_sum, shift_sum, col_sum = sums
+    slot = lax.broadcasted_iota(jnp.int32, (1, 4 * part), 1)
+    own = (slot >= tile[0] * part) & (slot < (tile[0] + 1) * part)
+    lone = jnp.where(tile[0] == 0, 1.0, 0.0).astype(F32)
+    vecs[0:1, :] = gain_sum
+    vecs[1:2, :] = shift_sum
+    for i in range(3):
+        piece = col_sum[:, i * part : (i + 1) * part]
+        vecs[2 + i : 3 + i, :] = jnp.where(own, jnp.concatenate([piece] * 4, axis=1), 0.0)
+    vecs[5:6, :] = bsum[...] * lone
+    vecs[6:8, :] = vec2[...]
+    vecs[8:9, :] = fb2[...] * lone
 
 
 def input_kernel(tile, m0, m1, m2, m3, w, x, rgrad, gain, out, ms, xs):
@@ -425,35 +437,42 @@
     store_tile(out, (rgrad[...] + norm_back(n, normed, inv, vec_row(gain))).astype(BF))
 
 
-def ffout_kernel(tile, p0, p1, p2, p3, fc1, fc2, ps):
-    rows = fc1.shape[0]
+def ffout_kernel(tile, a0, a1, a2, a3, b0, b1, b2, b3, fc1, fc2, ps):
     quarter = fc2.shape[0] // 4
-    for r, ref in enumerate((p0, p1, p2, p3)):
+    for r, ref in enumerate((a0, a1, a2, a3)):
         ps[r] = ref[...].astype(F32)
     for g in range(4):
         piece = ps[tile[0] ^ g]
         for i in range(fc1.shape[1] // (4 * quarter)):
             dst = (4 * i + g) * quarter
-            fc1[:, dst : dst + quarter] = piece[:rows, i * quarter : (i + 1) * quarter]
-        fc2[g * quarter : (g + 1) * quarter, :] = piece[rows:, :]
-
-
-def attnout_kernel(tile, p0, p1, p2, p3, gqkv, gout, vecs, ps):
-    rows = gqkv.shape[0]
-    width = gout.shape[1]
+            fc1[:, dst : dst + quarter] = piece[:, i * quarter : (i + 1) * quarter]
+    for r, ref in enumerate((b0, b1, b2, b3)):
+        ps[r, :quarter, :] = ref[...].astype(F32)
+    for g in range(4):
+        fc2[g * quarter : (g + 1) * quarter, :] = ps[tile[0] ^ g][:quarter]
+
+
+def attnout_kernel(tile, p0, p1, p2, p3, gqkv, gout, vecs, units, ps):
+    rows, width = gout.shape
     part = width // 4
+    quarter = units.shape[1] // 4
+    height = ps.shape[1] - rows
     for r, ref in enumerate((p0, p1, p2, p3)):
         ps[r] = ref[...].astype(F32)
     total = None
+    tails = []
     for g in range(4):
         piece = ps[tile[0] ^ g]
         for i in range(3):
             dst = i * width + g * part
             gqkv[:, dst : dst + part] = piece[:rows, i * part : (i + 1) * part]
         gout[:, g * part : (g + 1) * part] = piece[:rows, 3 * part :]
-        tail = piece[rows:, :]
+        tail = jnp.concatenate([piece[rows + j : rows + j + 1] for j in range(height)], axis=1)
         total = tail if g == 0 else total + tail
-    vecs[...] = total
+        tails.append(tail[:, 9 * rows : 9 * rows + quarter])
+    for i in range(9):
+        vecs[i : i + 1, :] = total[:, i * rows : (i + 1) * rows]
+    units[...] = jnp.concatenate(tails, axis=1)
 
 
 def body(
@@ -521,6 +540,7 @@
         us=13,
     )(at_tile, patch_mask, *x_blocks, norm1_gain, norm1_shift, w_own, b_own)
     ct_blocks, ctx = gather_tiles(cotangent, ctx)
+    later_tile, _ = tie(at_tile, ctx)
 
     fc1_own, fc1_b_own = pl.pallas_call(
         functools.partial(units_kernel, quarter=quarter),
@@ -537,7 +557,7 @@
         out_shape=[sds((width, units)), sds((1, units), F32)],
         cost_estimate=cost(4),
         name="units",
-    )(at_tile, fc1_weight, row(fc1_bias))
+    )(later_tile, fc1_weight, row(fc1_bias))
     fc2_own = lax.dynamic_index_in_dim(
         fc2_weight.reshape(imgs, 4, quarter, width), tile, 1, keepdims=False
     ).reshape(units, width)
@@ -625,60 +645,49 @@
         9,
         us=4,
     )(at_tile, *branch_blocks, out_weight, *ctx)
-    ff_bucket = jnp.concatenate(
-        [g1.reshape(imgs, share, units), g2.reshape(imgs, quarter, width)], axis=1
-    )
-    ff_start = start_imgs(ff_bucket, imgs)
+    direct = direct_sum(imgs)
+    g1 = g1.reshape(imgs, share, units)
+    g2 = g2.reshape(imgs, quarter, width)
+    if direct:
+        line = imgs // 2
+        near1 = exchange_near(g1.reshape(line, 2, share, units))
+        far2 = exchange_far(g2.reshape(line, 2, quarter, width))
     out_cols = [lax.dynamic_slice_in_dim(gout, (tile ^ r) * part, part, 1) for r in range(4)]
-    out_rows = scatter_tiles(out_cols)
-
-    *mixed, gqkv, msum, nsum = vec_call(
+    dctx, out_rows = tie(dctx, scatter_tiles(out_cols))
+    out_rows = jnp.concatenate(own_order(out_rows, tile), axis=0)
+
+    *mixed, gqkv, vecs = vec_call(
         functools.partial(attnback_kernel, cols=cols),
-        [sds((toks, 3 * part))] * 4
-        + [
-            sds((width, 3 * part)),
-            sds((1, 3 * part), F32),
-            sds((2, width), F32),
-        ],
-        7,
+        [sds((toks, 3 * part))] * 4 + [sds((width, 3 * part)), sds((9, width), F32)],
+        10,
         [
             pltpu.VMEM((part * HEADS // width, total, width // HEADS), F32),
             pltpu.VMEM((part * HEADS // width, total, width // HEADS), F32),
             pltpu.VMEM((total, 3 * part), BF),
         ],
         us=18,
-    )(at_tile, patch_mask, dctx, qkv, lse, hid1, nrm1, w_own)
+    )(at_tile, patch_mask, dctx, qkv, lse, hid1, nrm1, w_own, bsum, vec2, fb2)
     mixed_in = scatter_tiles(mixed)
-    out_rows, (gqkv,) = tie(out_rows, (gqkv,))
-    out_rows = own_order(out_rows, tile)
-
-    lone = (tile == 0).astype(F32)
-    fb1_row = lax.dynamic_update_index_in_dim(
-        jnp.zeros((imgs, 4, quarter), F32), fb1.reshape(imgs, quarter), tile, 1
-    )
-    heads_row = lax.dynamic_update_index_in_dim(
-        jnp.zeros((3, 4, part), F32), msum.reshape(3, part), tile, 1
-    ).reshape(3, width)
-    vec_rows = [nsum, heads_row, bsum * lone, vec2, fb2 * lone]
-    vecs = jnp.concatenate(vec_rows, axis=0).reshape(9, imgs, share).transpose(1, 0, 2)
-    vecs = jnp.concatenate(
-        [vecs.reshape(imgs, 9 * share), fb1_row.reshape(imgs, 4 * quarter)], axis=1
-    ).astype(BF)
-    count = vecs.shape[1]
+
+    vecs = vecs.reshape(9, imgs, share).transpose(1, 0, 2).reshape(imgs, 9 * share)
+    count = 9 * share + quarter
     vec_height = -(-count // width)
-    vecs = jnp.pad(vecs, ((0, 0), (0, vec_height * width - count)))
+    spare = jnp.zeros((imgs, vec_height * width - count), F32)
+    vecs = jnp.concatenate([vecs, fb1.reshape(imgs, quarter), spare], axis=1).astype(BF)
     at_bucket = jnp.concatenate(
         [
-            jnp.concatenate([gqkv, jnp.concatenate(out_rows, axis=0)], axis=1).reshape(
-                imgs, share, width
-            ),
+            jnp.concatenate([gqkv, out_rows], axis=1).reshape(imgs, share, width),
             vecs.reshape(imgs, vec_height, width),
         ],
         axis=1,
     )
-    at_start = start_imgs(at_bucket, imgs)
-    ff_start, (mixed_in[0],) = tie(ff_start, (mixed_in[0],))
-    ff_sum = finish_imgs(ff_start, imgs, BF)
+    if direct:
+        near3 = exchange_near(at_bucket.reshape(line, 2, share + vec_height, width))
+        (near1, far2), (at_bucket,) = tie((near1, far2), (at_bucket,))
+        far1 = exchange_far(total_of(near1).astype(BF))
+        near2 = exchange_near(total_of(far2).astype(BF)[None])
+        near3, (far1[0],) = tie(near3, (far1[0],))
+        far3 = exchange_far(total_of(near3).astype(BF))
 
     patches_grad = vec_call(
         input_kernel,
@@ -688,41 +697,50 @@
         us=5,
     )(at_tile, *mixed_in, qkv_weight, patches, rgrad, norm1_gain)
 
-    at_start, (patches_grad, ff_sum) = tie(at_start, (patches_grad, ff_sum))
-    ff_pieces, _ = gather_tiles(ff_sum.astype(BF))
-    at_sum = finish_imgs(at_start, imgs, BF)
+    if direct:
+        fc2_sum = total_of(near2)[0].astype(BF)
+        fc1_sum = total_of(far1).astype(BF)
+        far3, (fc1_sum, fc2_sum, patches_grad) = tie(far3, (fc1_sum, fc2_sum, patches_grad))
+        at_sum = total_of(far3).astype(BF)
+    else:
+        fc1_sum, fc2_sum, at_sum = (plain_sum(b) for b in (g1, g2, at_bucket))
+    fc1_pieces, _ = gather_tiles(fc1_sum)
+    fc2_pieces, _ = gather_tiles(fc2_sum)
     fc1_grad, fc2_grad = vec_call(
         ffout_kernel,
         [sds((share, ff), F32), sds((4 * quarter, width), F32)],
-        4,
-        [pltpu.VMEM((4, share + quarter, width), F32)],
+        8,
+        [pltpu.VMEM((4, max(share, quarter), width), F32)],
         us=3,
-    )(at_tile, *ff_pieces)
-    at_pieces, (fc1_grad, fc2_grad) = gather_tiles(at_sum.astype(BF), (fc1_grad, fc2_grad))
-    qkv_grad, out_grad, vec_sum = vec_call(
+    )(at_tile, *fc1_pieces, *fc2_pieces)
+    at_pieces, (fc1_grad, fc2_grad) = gather_tiles(at_sum, (fc1_grad, fc2_grad))
+    qkv_grad, out_grad, vec_sum, unit_sum = vec_call(
         attnout_kernel,
-        [sds((share, 3 * width), F32), sds((share, width), F32), sds((vec_height, width), F32)],
+        [
+            sds((share, 3 * width), F32),
+            sds((share, width), F32),
+            sds((9, share), F32),
+            sds((1, 4 * quarter), F32),
+        ],
         4,
         [pltpu.VMEM((4, share + vec_height, width), F32)],
         us=3,
     )(at_tile, *at_pieces)
-    v = vec_sum.reshape(-1)
-    piece = [v[i * share : (i + 1) * share] for i in range(9)]
     return (
         layer_out,
         patches_grad,
-        piece[0],
-        piece[1],
+        vec_sum[0],
+        vec_sum[1],
         qkv_grad,
-        jnp.stack([piece[2], piece[4]], axis=1),
+        jnp.stack([vec_sum[2], vec_sum[4]], axis=1),
         out_grad,
-        piece[5],
-        piece[6],
-        piece[7],
+        vec_sum[5],
+        vec_sum[6],
+        vec_sum[7],
         fc1_grad,
-        v[9 * share : count],
+        unit_sum.reshape(-1),
         fc2_grad,
-        piece[8],
+        vec_sum[8],
     )
 
 

time: 193 us -> 174 us (0.902)
  starting transfers between devices: 54.8 us -> 31.4 us
  waiting for transfers between devices: 29.7 us -> 39 us
  other arithmetic: 11.1 us -> 6.96 us
    ppermute x14 -> x12, starting transfers between devices: 39.2 us -> 12.7 us  [the longest x9 8.9 us: exchange_far(): lax.ppermute(send, 'imgs', [(i, i ^ 2 * k) for i in range(count)])]
    ppermute x9 -> x10, waiting for transfers between devices: 6.19 us -> 17.8 us  [to_peer(): return lax.ppermute(value, 'rows', [(0, 1), (1, 0)])]
    ppermute x14 -> x12, waiting for transfers between devices: 19.5 us -> 12 us  [the longest x9 12 us: exchange_far(): lax.ppermute(send, 'imgs', [(i, i ^ 2 * k) for i in range(count)])]
    ppermute x3, waiting for transfers between devices: 1.49 us -> 7.77 us  [to_peer(): return lax.ppermute(value, GROUP, [(i, i ^ 3) for i in range(4)])]
    squeeze x0 -> x6, local copies, waits for them, and re-layouts: none -> 4.65 us  [the longest x2 2.28 us: exchange_near(): send = lax.dynamic_index_in_dim(parts, 1 - side, 1, keepdims=False)]
    ppermute x9 -> x10, starting transfers between devices: 10.1 us -> 13.8 us  [to_peer(): return lax.ppermute(value, 'rows', [(0, 1), (1, 0)])]
    squeeze x1 -> x0, other arithmetic: 2.78 us -> none  [start_imgs(): send = lax.dynamic_index_in_dim(split, 1 - side, 1, keepdims=False)]
    convert_element_type x9 -> x6, other arithmetic: 3.65 us -> 4.7 us  [the longest x1 1.29 us: body(): near2 = exchange_near(total_of(far2).astype(BF)[None])]
  transfers between devices with their start and end apart: 41 -> 42, of which waited for: 15 -> 14; matrix products, arithmetic and copies ran while one was open for 9% -> 8% of each run, Pallas kernels for 38% -> 42%
where the time goes in v1:
time: 174 us
  Pallas kernels  78.4 us (45%)
  waiting for transfers between devices  39 us (22%)
  starting transfers between devices  31.4 us (18%)
  local copies, waits for them, and re-layouts  16.8 us (10%)
  other arithmetic  6.96 us (4%)
    pallas_call x1, Pallas kernels, body(): vec_call(functools.partial(attnback_kernel, cols=cols), [sds((toks, 3 * p...  19.2 us
    ppermute x10, waiting for transfers between devices, to_peer(): return lax.ppermute(value, 'rows', [(0, 1), (1, 0)])  17.8 us
    ppermute x10, starting transfers between devices, to_peer(): return lax.ppermute(value, 'rows', [(0, 1), (1, 0)])  13.8 us
    pallas_call x1, Pallas kernels, body(): vec_call(attn_kernel, [sds((total, width)), sds((total, width)), sds((tot...  13.6 us
    ppermute x9, waiting for transfers between devices, exchange_far(): lax.ppermute(send, 'imgs', [(i, i ^ 2 * k) for i in range(count)])  12 us
    pallas_call x1, Pallas kernels, body(): pl.pallas_call(mlp_kernel, grid=(chunks,), in_specs=[SMEM, whole(*patch_m...  10.5 us
    pallas_call x1, Pallas kernels, body(): vec_call(ffgrad_kernel, [sds((width, units)), sds((units, width)), sds((1...  9.04 us
    ppermute x9, starting transfers between devices, exchange_far(): lax.ppermute(send, 'imgs', [(i, i ^ 2 * k) for i in range(count)])  8.9 us
  transfers between devices with their start and end apart: 42, of which 14 were waited for; matrix products, arithmetic and copies ran while one was open for 8% of the time, Pallas kernels for 42%

profile of v1, /device:TPU:0, one launch (start us, length us, event | category | flops | bytes accessed | tf_op | source)
XLA Modules:
  0.0 173.6 jit_solution(2720327186699602392)
XLA Ops:
  0.6 3.0 %collective-permute-start.2 = (bf16[1,15,15,768]{3,2,1,0:T(8,128)(2,1)}, bf16[1,15,15,768]{3,2,1,0:T(8,128)(2,1)S(1)}, u32[]{:S(2)}, u32[]{:S(2)}) collective-permute-start(bf16[1,15,15,768]{3,2,1,0:T(8,128)(2,1)} %x.3), channel_id=1, source_target_pairs={{0,16},{16,0},{1,17},{17,1},{2,18},{18,2},{3,19},{19,3},{4,20},{20... | collective-permute-start | bytes 1036808 | tf_op jit(solution)/shard_map/ppermute | solution.py:38
  3.7 4.1 %heads.1 = (bf16[768,576]{1,0:T(8,128)(2,1)}, f32[1,576]{1,0:T(1,128)}) custom-call(s32[1]{0:T(128)} %bitcast.tile, bf16[768,2304]{1,0:T(8,128)(2,1)} %w.1, f32[2,768]{1,0:T(2,128)} %bitcast.89), custom_call_target="tpu_custom_call" | custom-call | flops 4000000000 | bytes 4000000 | tf_op jit(solution)/shard_map/heads/pallas_call | solution.py:511
  7.8 4.7 %collective-permute-done.2.x2 = bf16[1,15,15,768]{3,2,1,0:T(8,128)(2,1)S(1)} collective-permute-done((bf16[1,15,15,768]{3,2,1,0:T(8,128)(2,1)}, bf16[1,15,15,768]{3,2,1,0:T(8,128)(2,1)S(1)}, u32[]{:S(2)}, u32[]{:S(2)}) %collective-permute-start.2) | collective-permute-done | bytes 345632 | tf_op jit(solution)/shard_map/ppermute | solution.py:38
  12.5 1.8 %collective-permute-start = (bf16[1,15,15,768]{3,2,1,0:T(8,128)(2,1)S(1)}, bf16[1,15,15,768]{3,2,1,0:T(8,128)(2,1)S(1)}, u32[]{:S(2)}, u32[]{:S(2)}) collective-permute-start(bf16[1,15,15,768]{3,2,1,0:T(8,128)(2,1)S(1)} %copy-done.9), channel_id=1, source_target_pairs={{0,16},{16,0},{1,17},{17,1},{2,18},{18,2},{3,19},{19,3},{4,20},{20... | collective-permute-start | bytes 1036808 | tf_op jit(solution)/shard_map/ppermute | solution.py:38
  14.9 2.4 %constant_dynamic-slice_fusion.5 = bf16[8,1,96,768]{3,2,1,0:T(8,128)(2,1)} fusion(bf16[8,4,96,768]{3,2,1,0:T(8,128)(2,1)} %bitcast.82, s32[]{:T(128)S(6)} %select_n.80), kind=kLoop, calls=%fused_computation.41 | loop fusion | bytes 2359300 | tf_op jit(solution)/shard_map/jit(dynamic_index_in_dim)/dynamic_slice | solution.py:561
  18.7 13.6 %shard_map.254 = (bf16[960,768]{1,0:T(8,128)(2,1)}, bf16[960,768]{1,0:T(8,128)(2,1)}, bf16[960,576]{1,0:T(8,128)(2,1)}, f32[960,128]{1,0:T(8,128)}, bf16[240,192...) custom-call(s32[1]{0:T(128)} %bitcast.tile, ...), custom_call_target="tpu_custom_call" | custom-call | flops 12999999488 | bytes 13000000 | tf_op jit(solution)/shard_map/pallas_call | solution.py:529
  34.3 4.5 %units.1 = (bf16[768,768]{1,0:T(8,128)(2,1)}, f32[1,768]{1,0:T(1,128)}) custom-call(s32[1]{0:T(128)} %bitcast.tile, bf16[768,3072]{1,0:T(8,128)(2,1)} %fc1.3, f32[1,3072]{1,0:T(1,128)} %bitcast.87), custom_call_target="tpu_custom_call" | custom-call | flops 4000000000 | bytes 4000000 | tf_op jit(solution)/shard_map/units/pallas_call | solution.py:545
  41.0 3.1 %shard_map.255 = (f32[240,768]{1,0:T(8,128)}, bf16[240,768]{1,0:T(8,128)(2,1)}) custom-call(s32[1]{0:T(128)} %bitcast.tile, bf16[240,192]{1,0:T(8,128)(2,1)} %get-tuple-element.112.c0, bf16[240,192]{1,0:T(8,128)(2,1)} %copy-done.34, bf16[240,192]{1,0:T(8,128)(2,1)} %copy-done.35, bf16[240,192]{1,0:T(8,128)(2,1)} %copy-done.36, bf16[768,768]{1,0:T(8,128)(2,1)} %wo.3, ...), custom_call_target="tpu_custom_call" | custom-call | flops 3000000000 | bytes 3000000 | tf_op jit(solution)/shard_map/pallas_call | solution.py:567
  44.6 10.5 %mlp.1 = (bf16[1,15,15,768]{3,2,1,0:T(8,128)(2,1)}, bf16[240,768]{1,0:T(8,128)(2,1)}, f32[240,768]{1,0:T(8,128)}, f32[2,768]{1,0:T(2,128)}) custom-call(s32[1]{0:T(128)} %bitcast.tile, s32[1,30,30]{2,1,0:T(8,128)} %copy.50.mask, f32[240,768]{1,0:T(8,128)} %get-tuple-element.116.resid, bf16[240,768]{1,0:T(8,128)(2,1)} %get-tuple-element.117.hid.h0, ...), custom_call_target="tpu_custom_call" | custom-call | flops 11000000512 | bytes 11000000 | tf_op jit(solution)/shard_map/mlp/pallas_call | solution.py:581
  59.7 9.0 %shard_map.256 = (bf16[768,768]{1,0:T(8,128)(2,1)}, bf16[768,768]{1,0:T(8,128)(2,1)}, f32[1,768]{1,0:T(1,128)}, f32[1,768]{1,0:T(1,128)}) custom-call(s32[1]{0:T(128)} %bitcast.tile, s32[1,30,30]{2,1,0:T(8,128)} %copy.50.mask, bf16[240,768]{1,0:T(8,128)(2,1)} %get-tuple-element.117.hid.h0, bf16[240,768]{1,0:T(8,128)(2,1)} %copy-done.16, ...), custom_call_target="tpu_custom_call" | custom-call | flops 8999999488 | bytes 9000000 | tf_op jit(solution)/shard_map/pallas_call | solution.py:629
  69.1 2.3 %dynamic-slice_bitcast_fusion = (bf16[4,96,768]{2,1,0:T(8,128)(2,1)}, bf16[4,96,768]{2,1,0:T(8,128)(2,1)S(1)}) fusion(bf16[4,2,96,768]{3,2,1,0:T(8,128)(2,1)} %bitcast.78, s32[]{:T(128)S(6)} %select_n.90, s32[]{:T(128)S(6)} %select_n.89), kind=kLoop, calls=%fused_computation.12 | loop fusion | bytes 2359304 | tf_op jit(solution)/shard_map/jit(dynamic_index_in_dim)/squeeze | solution.py:84
  73.8 3.6 %collective-permute-start.20 = (bf16[2,96,768]{2,1,0:T(8,128)(2,1)}, bf16[2,96,768]{2,1,0:T(8,128)(2,1)S(1)}, u32[]{:S(2)}, u32[]{:S(2)}) collective-permute-start(bf16[2,96,768]{2,1,0:T(8,128)(2,1)} %get-tuple-element.182), channel_id=1, source_target_pairs={{0,6},{1,7},{2,4},{3,5},{4,2},{5,3},{6,0},{7,1},{8,14},{9,15},{10,... | collective-permute-start | bytes 884744 | tf_op jit(solution)/shard_map/ppermute | solution.py:95
  77.4 3.5 %shard_map.257 = (bf16[960,192]{1,0:T(8,128)(2,1)}, bf16[192,768]{1,0:T(8,128)(2,1)}, f32[1,768]{1,0:T(1,128)}) custom-call(s32[1]{0:T(128)} %bitcast.tile, bf16[240,768]{1,0:T(8,128)(2,1)} %get-tuple-element.120.b0, bf16[240,768]{1,0:T(8,128)(2,1)} %collective-permute-done.8.b1, bf16[240,768]{1,0:T(8,128)(2,1)} %copy-done.11, ...), custom_call_target="tpu_custom_call" | custom-call | flops 4000000000 | bytes 4000000 | tf_op jit(solution)/shard_map/pallas_call | solution.py:642
  84.3 3.7 %collective-permute-done.16 = bf16[192,192]{1,0:T(8,128)(2,1)S(1)} collective-permute-done((bf16[192,192]{1,0:T(8,128)(2,1)S(1)}, bf16[192,192]{1,0:T(8,128)(2,1)S(1)}, u32[]{:S(2)}, u32[]{:S(2)}) %collective-permute-start.16) | collective-permute-done | bytes 73760 | tf_op jit(solution)/shard_map/ppermute | solution.py:38
  89.0 19.2 %shard_map.258 = (bf16[240,576]{1,0:T(8,128)(2,1)}, bf16[240,576]{1,0:T(8,128)(2,1)}, bf16[240,576]{1,0:T(8,128)(2,1)}, bf16[240,576]{1,0:T(8,128)(2,1)}, bf16[768,576]{1,0:T(8,128)(2,1)}, /*index=5*/f32[9,768]{1,0:T(8,128)}) custom-call(s32[1]{0:T(128)} %bitcast.tile, s32[1,30,30]{2,1,0:T(8,128)} %copy.50.mask, bf16[960,192]{1,0:T(8,128)(2,1)} %get-tuple-element.131.dctx, ...), custom_call_target="tpu_custom_call" | custom-call | flops 17999998976 | bytes 18000000 | tf_op jit(solution)/shard_map/pallas_call | solution.py:659
  117.7 3.0 %collective-permute-done.31.m2 = bf16[240,576]{1,0:T(8,128)(2,1)S(1)} collective-permute-done((bf16[240,576]{1,0:T(8,128)(2,1)S(1)}, bf16[240,576]{1,0:T(8,128)(2,1)S(1)}, u32[]{:S(2)}, u32[]{:S(2)}) %collective-permute-start.31) | collective-permute-done | bytes 276512 | tf_op jit(solution)/shard_map/ppermute | solution.py:38
  120.8 5.4 %collective-permute-done.32.m3 = bf16[240,576]{1,0:T(8,128)(2,1)S(1)} collective-permute-done((bf16[240,576]{1,0:T(8,128)(2,1)S(1)}, bf16[240,576]{1,0:T(8,128)(2,1)S(1)}, u32[]{:S(2)}, u32[]{:S(2)}) %collective-permute-start.32) | collective-permute-done | bytes 276512 | tf_op jit(solution)/shard_map/ppermute | solution.py:39
  126.8 4.9 %shard_map.259 = bf16[1,15,15,768]{3,2,1,0:T(8,128)(2,1)} custom-call(s32[1]{0:T(128)} %bitcast.tile, bf16[240,576]{1,0:T(8,128)(2,1)} %get-tuple-element.157.m0, bf16[240,576]{1,0:T(8,128)(2,1)} %collective-permute-done.30.m1, bf16[240,576]{1,0:T(8,128)(2,1)} %copy-done.23, bf16[240,576]{1,0:T(8,128)(2,1)} %copy-done.24, bf16[768,2304]{1,0:T(8,128)(2,1)} %w.1, ...), custom_call_target="tpu_custom_call" | custom-call | flops 5000000000 | bytes 5000000 | tf_op jit(solution)/shard_map/pallas_call | solution.py:692
  133.9 1.9 %collective-permute-start.24 = (bf16[98,768]{1,0:T(8,128)(2,1)S(1)}, bf16[98,768]{1,0:T(8,128)(2,1)S(1)}, u32[]{:S(2)}, u32[]{:S(2)}) collective-permute-start(bf16[98,768]{1,0:T(8,128)(2,1)S(1)} %get-tuple-element.187), channel_id=1, source_target_pairs={{0,4},{1,5},{2,6},{3,7},{4,0},{5,1},{6,2},{7,3},{8,12},{9,13},{10,... | collective-permute-start | bytes 451592 | tf_op jit(solution)/shard_map/ppermute | solution.py:95
  138.5 3.4 %collective-permute-done.23 = bf16[98,768]{1,0:T(8,128)(2,1)S(1)} collective-permute-done((bf16[98,768]{1,0:T(8,128)(2,1)S(1)}, bf16[98,768]{1,0:T(8,128)(2,1)S(1)}, u32[]{:S(2)}, u32[]{:S(2)}) %collective-permute-start.23) | collective-permute-done | bytes 150560 | tf_op jit(solution)/shard_map/ppermute | solution.py:95
  141.9 8.6 %collective-permute-done.24 = bf16[98,768]{1,0:T(8,128)(2,1)S(1)} collective-permute-done((bf16[98,768]{1,0:T(8,128)(2,1)S(1)}, bf16[98,768]{1,0:T(8,128)(2,1)S(1)}, u32[]{:S(2)}, u32[]{:S(2)}) %collective-permute-start.24) | collective-permute-done | bytes 150560 | tf_op jit(solution)/shard_map/ppermute | solution.py:95
  153.0 4.2 %collective-permute-done.36.a2 = bf16[96,768]{1,0:T(8,128)(2,1)S(1)} collective-permute-done((bf16[96,768]{1,0:T(8,128)(2,1)S(1)}, bf16[96,768]{1,0:T(8,128)(2,1)S(1)}, u32[]{:S(2)}, u32[]{:S(2)}) %collective-permute-start.36) | collective-permute-done | bytes 147488 | tf_op jit(solution)/shard_map/ppermute | solution.py:38
  162.3 3.4 %shard_map.260 = (f32[96,3072]{1,0:T(8,128)}, f32[384,768]{1,0:T(8,128)}) custom-call(s32[1]{0:T(128)} %bitcast.tile, bf16[96,768]{1,0:T(8,128)(2,1)} %copy-done.5, bf16[96,768]{1,0:T(8,128)(2,1)} %copy-done.30, bf16[96,768]{1,0:T(8,128)(2,1)} %copy-done.28, bf16[96,768]{1,0:T(8,128)(2,1)} %copy-done.32, bf16[96,768]{1,0:T(8,128)(2,1)} %copy-done.4, ...), custom_call_target="tpu_custom_call" | custom-call | flops 3000000000 | bytes 3000000 | tf_op jit(solution)/shard_map/pallas_call | solution.py:709
  167.8 2.5 %shard_map.261 = (f32[96,2304]{1,0:T(8,128)}, f32[96,768]{1,0:T(8,128)}, f32[9,96]{1,0:T(8,128)}, f32[1,384]{1,0:T(1,128)}) custom-call(s32[1]{0:T(128)} %bitcast.tile, bf16[98,768]{1,0:T(8,128)(2,1)} %copy-done.3, bf16[98,768]{1,0:T(8,128)(2,1)} %copy-done.26, bf16[98,768]{1,0:T(8,128)(2,1)} %copy-done.25, bf16[98,768]{1,0:T(8,128)(2,1)} %copy-done.27), custom_call_target="tpu_custom_call" | custom-call | flops 3000000000 | bytes 3000000 | tf_op jit(solution)/shard_map/pallas_call | solution.py:717
  (176 shorter events, 46.3 us)
Async XLA Ops:
  0.6 11.8 %collective-permute-start.2 = (bf16[1,15,15,768]{3,2,1,0:T(8,128)(2,1)}, bf16[1,15,15,768]{3,2,1,0:T(8,128)(2,1)S(1)}, u32[]{:S(2)}, u32[]{:S(2)}) collective-permute-start(bf16[1,15,15,768]{3,2,1,0:T(8,128)(2,1)} %x.3), channel_id=1, source_target_pairs={{0,16},{16,0},{1,17},{17,1},{2,18},{18,2},{3,19},{19,3},{4,20},{20... | collective-permute-start | bytes 1036808 | tf_op jit(solution)/shard_map/ppermute | solution.py:38
  3.7 13.6 %collective-permute-start.1 = (bf16[1,15,15,768]{3,2,1,0:T(8,128)(2,1)}, bf16[1,15,15,768]{3,2,1,0:T(8,128)(2,1)S(1)}, u32[]{:S(2)}, u32[]{:S(2)}) collective-permute-start(bf16[1,15,15,768]{3,2,1,0:T(8,128)(2,1)} %x.3), channel_id=1, source_target_pairs={{0,8},{8,0},{1,9},{9,1},{2,10},{10,2},{3,11},{11,3},{4,12},{12,4},... | collective-permute-start | bytes 1036808 | tf_op jit(solution)/shard_map/ppermute | solution.py:36
  12.5 19.9 %collective-permute-start = (bf16[1,15,15,768]{3,2,1,0:T(8,128)(2,1)S(1)}, bf16[1,15,15,768]{3,2,1,0:T(8,128)(2,1)S(1)}, u32[]{:S(2)}, u32[]{:S(2)}) collective-permute-start(bf16[1,15,15,768]{3,2,1,0:T(8,128)(2,1)S(1)} %copy-done.9), channel_id=1, source_target_pairs={{0,16},{16,0},{1,17},{17,1},{2,18},{18,2},{3,19},{19,3},{4,20},{20... | collective-permute-start | bytes 1036808 | tf_op jit(solution)/shard_map/ppermute | solution.py:38
  44.2 11.1 %collective-permute-start.7 = (bf16[240,768]{1,0:T(8,128)(2,1)}, bf16[240,768]{1,0:T(8,128)(2,1)S(1)}, u32[]{:S(2)}, u32[]{:S(2)}) collective-permute-start(bf16[240,768]{1,0:T(8,128)(2,1)} %get-tuple-element.117.hid.h0), channel_id=1, source_target_pairs={{0,16},{16,0},{1,17},{17,1},{2,18},{18,2},{3,19},{19,3},{4,20},{20... | collective-permute-start | bytes 1105928 | tf_op jit(solution)/shard_map/ppermute | solution.py:38
  44.5 13.6 %collective-permute-start.10 = (bf16[240,768]{1,0:T(8,128)(2,1)}, bf16[240,768]{1,0:T(8,128)(2,1)S(1)}, u32[]{:S(2)}, u32[]{:S(2)}) collective-permute-start(bf16[240,768]{1,0:T(8,128)(2,1)} %get-tuple-element.117.hid.h0), channel_id=1, source_target_pairs={{0,8},{8,0},{1,9},{9,1},{2,10},{10,2},{3,11},{11,3},{4,12},{12,4},... | collective-permute-start | bytes 1105928 | tf_op jit(solution)/shard_map/ppermute | solution.py:36
  56.1 12.6 %collective-permute-start.9 = (bf16[240,768]{1,0:T(8,128)(2,1)}, bf16[240,768]{1,0:T(8,128)(2,1)S(1)}, u32[]{:S(2)}, u32[]{:S(2)}) collective-permute-start(bf16[240,768]{1,0:T(8,128)(2,1)} %get-tuple-element.120.b0), channel_id=1, source_target_pairs={{0,16},{16,0},{1,17},{17,1},{2,18},{18,2},{3,19},{19,3},{4,20},{20... | collective-permute-start | bytes 1105928 | tf_op jit(solution)/shard_map/ppermute | solution.py:38
  57.8 19.6 %collective-permute-start.8 = (bf16[240,768]{1,0:T(8,128)(2,1)}, bf16[240,768]{1,0:T(8,128)(2,1)}, u32[]{:S(2)}, u32[]{:S(2)}) collective-permute-start(bf16[240,768]{1,0:T(8,128)(2,1)} %get-tuple-element.120.b0), channel_id=1, source_target_pairs={{0,8},{8,0},{1,9},{9,1},{2,10},{10,2},{3,11},{11,3},{4,12},{12,4},... | collective-permute-start | bytes 1105928 | tf_op jit(solution)/shard_map/ppermute | solution.py:36
  68.7 8.7 %collective-permute-start.14 = (bf16[240,768]{1,0:T(8,128)(2,1)S(1)}, bf16[240,768]{1,0:T(8,128)(2,1)}, u32[]{:S(2)}, u32[]{:S(2)}) collective-permute-start(bf16[240,768]{1,0:T(8,128)(2,1)S(1)} %collective-permute-done.9.b2), channel_id=1, source_target_pairs={{0,8},{8,0},{1,9},{9,1},{2,10},{10,2},{3,11},{11,3},{4,12},{12,4},... | collective-permute-start | bytes 1105928 | tf_op jit(solution)/shard_map/ppermute | solution.py:36
  71.3 41.5 %collective-permute-start.19 = (bf16[4,96,768]{2,1,0:T(8,128)(2,1)}, bf16[4,96,768]{2,1,0:T(8,128)(2,1)}, u32[]{:S(2)}, u32[]{:S(2)}) collective-permute-start(bf16[4,96,768]{2,1,0:T(8,128)(2,1)} %get-tuple-element.184), channel_id=1, source_target_pairs={{0,1},{1,0},{2,3},{3,2},{4,5},{5,4},{6,7},{7,6},{8,9},{9,8},{10,11... | collective-permute-start | bytes 1769480 | tf_op jit(solution)/shard_map/ppermute | solution.py:86
  73.8 36.2 %collective-permute-start.20 = (bf16[2,96,768]{2,1,0:T(8,128)(2,1)}, bf16[2,96,768]{2,1,0:T(8,128)(2,1)S(1)}, u32[]{:S(2)}, u32[]{:S(2)}) collective-permute-start(bf16[2,96,768]{2,1,0:T(8,128)(2,1)} %get-tuple-element.182), channel_id=1, source_target_pairs={{0,6},{1,7},{2,4},{3,5},{4,2},{5,3},{6,0},{7,1},{8,14},{9,15},{10,... | collective-permute-start | bytes 884744 | tf_op jit(solution)/shard_map/ppermute | solution.py:95
  84.2 27.9 %collective-permute-start.21 = (bf16[2,96,768]{2,1,0:T(8,128)(2,1)S(1)}, bf16[2,96,768]{2,1,0:T(8,128)(2,1)}, u32[]{:S(2)}, u32[]{:S(2)}) collective-permute-start(bf16[2,96,768]{2,1,0:T(8,128)(2,1)S(1)} %get-tuple-element.181), channel_id=1, source_target_pairs={{0,4},{1,5},{2,6},{3,7},{4,0},{5,1},{6,2},{7,3},{8,12},{9,13},{10,... | collective-permute-start | bytes 884744 | tf_op jit(solution)/shard_map/ppermute | solution.py:95
  88.0 24.3 %collective-permute-start.22 = (bf16[2,96,768]{2,1,0:T(8,128)(2,1)S(1)}, bf16[2,96,768]{2,1,0:T(8,128)(2,1)}, u32[]{:S(2)}, u32[]{:S(2)}) collective-permute-start(bf16[2,96,768]{2,1,0:T(8,128)(2,1)S(1)} %get-tuple-element.180), channel_id=1, source_target_pairs={{0,2},{1,3},{2,0},{3,1},{4,6},{5,7},{6,4},{7,5},{8,10},{9,11},{10,... | collective-permute-start | bytes 884744 | tf_op jit(solution)/shard_map/ppermute | solution.py:95
  108.2 8.8 %collective-permute-start.30 = (bf16[240,576]{1,0:T(8,128)(2,1)}, bf16[240,576]{1,0:T(8,128)(2,1)}, u32[]{:S(2)}, u32[]{:S(2)}) collective-permute-start(bf16[240,576]{1,0:T(8,128)(2,1)} %get-tuple-element.158), channel_id=1, source_target_pairs={{0,8},{8,0},{1,9},{9,1},{2,10},{10,2},{3,11},{11,3},{4,12},{12,4},... | collective-permute-start | bytes 829448 | tf_op jit(solution)/shard_map/ppermute | solution.py:36
  110.6 10.1 %collective-permute-start.31 = (bf16[240,576]{1,0:T(8,128)(2,1)S(1)}, bf16[240,576]{1,0:T(8,128)(2,1)S(1)}, u32[]{:S(2)}, u32[]{:S(2)}) collective-permute-start(bf16[240,576]{1,0:T(8,128)(2,1)S(1)} %copy-done.22), channel_id=1, source_target_pairs={{0,16},{16,0},{1,17},{17,1},{2,18},{18,2},{3,19},{19,3},{4,20},{20... | collective-permute-start | bytes 829448 | tf_op jit(solution)/shard_map/ppermute | solution.py:38
  112.1 14.0 %collective-permute-start.32 = (bf16[240,576]{1,0:T(8,128)(2,1)S(1)}, bf16[240,576]{1,0:T(8,128)(2,1)S(1)}, u32[]{:S(2)}, u32[]{:S(2)}) collective-permute-start(bf16[240,576]{1,0:T(8,128)(2,1)S(1)} %copy-done.21), channel_id=1, source_target_pairs={{0,24},{8,16},{16,8},{24,0},{1,25},{9,17},{17,9},{25,1},{2,26},{10... | collective-permute-start | bytes 829448 | tf_op jit(solution)/shard_map/ppermute | solution.py:39
  112.3 20.4 %collective-permute-start.18 = (bf16[4,98,768]{2,0,1:T(4,128)(2,1)S(1)}, bf16[4,98,768]{2,0,1:T(4,128)(2,1)S(1)}, u32[]{:S(2)}, u32[]{:S(2)}) collective-permute-start(bf16[4,98,768]{2,0,1:T(4,128)(2,1)S(1)} %bitcast.80), channel_id=1, source_target_pairs={{0,1},{1,0},{2,3},{3,2},{4,5},{5,4},{6,7},{7,6},{8,9},{9,8},{10,11... | collective-permute-start | bytes 1806344 | tf_op jit(solution)/shard_map/ppermute | solution.py:86
  114.2 17.6 %collective-permute-start.29 = (bf16[1,96,768]{2,1,0:T(8,128)(2,1)S(1)}, bf16[1,96,768]{2,1,0:T(8,128)(2,1)}, u32[]{:S(2)}, u32[]{:S(2)}) collective-permute-start(bf16[1,96,768]{2,1,0:T(8,128)(2,1)S(1)} %constant_dynamic-slice_fusion), channel_id=1, source_target_pairs={{0,1},{1,0},{2,3},{3,2},{4,5},{5,4},{6,7},{7,6},{8,9},{9,8},{10,11... | collective-permute-start | bytes 442376 | tf_op jit(solution)/shard_map/ppermute | solution.py:86
  117.0 18.7 %collective-permute-start.26 = (bf16[96,768]{1,0:T(8,128)(2,1)S(1)}, bf16[96,768]{1,0:T(8,128)(2,1)S(1)}, u32[]{:S(2)}, u32[]{:S(2)}) collective-permute-start(bf16[96,768]{1,0:T(8,128)(2,1)S(1)} %get-tuple-element.190), channel_id=1, source_target_pairs={{0,6},{1,7},{2,4},{3,5},{4,2},{5,3},{6,0},{7,1},{8,14},{9,15},{10,... | collective-permute-start | bytes 442376 | tf_op jit(solution)/shard_map/ppermute | solution.py:95
  120.8 16.6 %collective-permute-start.27 = (bf16[96,768]{1,0:T(8,128)(2,1)S(1)}, bf16[96,768]{1,0:T(8,128)(2,1)}, u32[]{:S(2)}, u32[]{:S(2)}) collective-permute-start(bf16[96,768]{1,0:T(8,128)(2,1)S(1)} %get-tuple-element.192), channel_id=1, source_target_pairs={{0,4},{1,5},{2,6},{3,7},{4,0},{5,1},{6,2},{7,3},{8,12},{9,13},{10,... | collective-permute-start | bytes 442376 | tf_op jit(solution)/shard_map/ppermute | solution.py:95
  126.1 11.3 %collective-permute-start.28 = (bf16[96,768]{1,0:T(8,128)(2,1)S(1)}, bf16[96,768]{1,0:T(8,128)(2,1)}, u32[]{:S(2)}, u32[]{:S(2)}) collective-permute-start(bf16[96,768]{1,0:T(8,128)(2,1)S(1)} %get-tuple-element.191), channel_id=1, source_target_pairs={{0,2},{1,3},{2,0},{3,1},{4,6},{5,7},{6,4},{7,5},{8,10},{9,11},{10,... | collective-permute-start | bytes 442376 | tf_op jit(solution)/shard_map/ppermute | solution.py:95
  132.9 9.0 %collective-permute-start.23 = (bf16[98,768]{1,0:T(8,128)(2,1)S(1)}, bf16[98,768]{1,0:T(8,128)(2,1)S(1)}, u32[]{:S(2)}, u32[]{:S(2)}) collective-permute-start(bf16[98,768]{1,0:T(8,128)(2,1)S(1)} %get-tuple-element.188), channel_id=1, source_target_pairs={{0,6},{1,7},{2,4},{3,5},{4,2},{5,3},{6,0},{7,1},{8,14},{9,15},{10,... | collective-permute-start | bytes 451592 | tf_op jit(solution)/shard_map/ppermute | solution.py:95
  133.9 16.6 %collective-permute-start.24 = (bf16[98,768]{1,0:T(8,128)(2,1)S(1)}, bf16[98,768]{1,0:T(8,128)(2,1)S(1)}, u32[]{:S(2)}, u32[]{:S(2)}) collective-permute-start(bf16[98,768]{1,0:T(8,128)(2,1)S(1)} %get-tuple-element.187), channel_id=1, source_target_pairs={{0,4},{1,5},{2,6},{3,7},{4,0},{5,1},{6,2},{7,3},{8,12},{9,13},{10,... | collective-permute-start | bytes 451592 | tf_op jit(solution)/shard_map/ppermute | solution.py:95
  135.8 14.7 %collective-permute-start.25 = (bf16[98,768]{1,0:T(8,128)(2,1)S(1)}, bf16[98,768]{1,0:T(8,128)(2,1)S(1)}, u32[]{:S(2)}, u32[]{:S(2)}) collective-permute-start(bf16[98,768]{1,0:T(8,128)(2,1)S(1)} %get-tuple-element.186), channel_id=1, source_target_pairs={{0,2},{1,3},{2,0},{3,1},{4,6},{5,7},{6,4},{7,5},{8,10},{9,11},{10,... | collective-permute-start | bytes 451592 | tf_op jit(solution)/shard_map/ppermute | solution.py:95
  152.5 8.4 %collective-permute-start.38 = (bf16[96,768]{1,0:T(8,128)(2,1)S(1)}, bf16[96,768]{1,0:T(8,128)(2,1)S(1)}, u32[]{:S(2)}, u32[]{:S(2)}) collective-permute-start(bf16[96,768]{1,0:T(8,128)(2,1)S(1)} %fusion.3.b0), channel_id=1, source_target_pairs={{0,8},{8,0},{1,9},{9,1},{2,10},{10,2},{3,11},{11,3},{4,12},{12,4},... | collective-permute-start | bytes 442376 | tf_op jit(solution)/shard_map/ppermute | solution.py:36
  (55 other events, 250.0 us)
